TPU v7x, 512 devices: a whole 4x4x16 slice. The times are simulated.
512 devices in a mesh: space: 64 (over z, y_lo, core), kgrp: 8 (over y_hi, x).
Axes of the slice: x: 4, y: 4 (y_hi: 2, y_lo: 2; y = y_hi * 2 + y_lo), z: 16, core: 2. Of those that a mesh axis runs over, the one named last changes fastest.
Arguments:
- features: bfloat16 [65536, 128], P(('space', 'kgrp')), may hold values from -8 to 8, as said below
- positions: float32 [65536, 3], P('space'), may hold values from 0 to 8192, as said below
- wave_index: int32 [6144, 3], P('kgrp'), may hold values from -12 to 12, as said below
- wave_filter: float32 [6144, 128], P('kgrp'), may hold values from 0.2 to 2
- mix_pair: bfloat16 [2, 128, 128], replicated, may hold values from -0.5 to 0.5
- msg_weight: bfloat16 [128, 128], replicated, may hold values from -0.5 to 0.5
- chan_width: float32 [128], replicated, may hold values from 1 to 30
- pair_dist: float32 [65536, 16], P(('space', 'kgrp')), may hold values from 1 to 25
- neighbours: int32 [65536, 16], P(('space', 'kgrp')), may hold values from 0 to 191, as said below
- norm_gain: float32 [128], replicated, may hold values from 0.1 to 1.9
- in_weight: bfloat16 [128, 512], replicated, may hold values from -0.5 to 0.5
- out_weight: bfloat16 [512, 128], replicated, may hold values from -0.25 to 0.25
Outputs:
- updated: bfloat16 [65536, 128], P(('space', 'kgrp'))
Inputs may be any that keep to these rules, and one draw needn't show every extreme that they name: Entries of the features are clipped to the range. `positions`: x and y lie in [0, 16); atom i has z in [i / 8, (i + 1) / 8). `wave_index`: the wave vectors are distinct and nonzero, one of each plus-minus k pair: each is lexicographically positive (first nonzero component positive). Rows of a device's extended block are its lower 32 wrapped neighbours' rows, its own 128 rows, then 32 upper ones; an atom at own row r lists rows r + 32 + o with 1 <= |o| <= 32.
All inputs are finite; a program needn't handle non-finite values.
Results may differ from a plain program's by a relative error of at most 0.008.
Values may be sent and summed in bfloat16 or wider, within the bound.
A program may use at most 64 MiB of HBM per device.

v0:
```python
import math

import jax
import jax.numpy as jnp
from jax import lax
from jax.sharding import PartitionSpec as P

box_side = 16.0
slab_step = 0.125
two_pi = 2.0 * math.pi


def padded(shard, sides, width):
    for axis, dim in sides:
        size, length = (lax.axis_size(axis), shard.shape[dim])
        up = [(i, (i + 1) % size) for i in range(size)]
        down = [(j, i) for i, j in up]
        last = lax.slice_in_dim(shard, length - width, length, axis=dim)
        first = lax.slice_in_dim(shard, 0, width, axis=dim)
        before = lax.ppermute(last, axis, up)
        after = lax.ppermute(first, axis, down)
        shard = jnp.concatenate([before, shard, after], axis=dim)
    return shard


def wave_vectors(wave_index, slab_length):
    counts = wave_index.astype(jnp.float32)
    return jnp.stack(
        [
            counts[:, 0] * (two_pi / box_side),
            counts[:, 1] * (two_pi / box_side),
            counts[:, 2] * (two_pi / slab_length),
        ],
        axis=0,
    )


def phase_angles(points, wave_vecs):
    return (
        points[:, 0:1] * wave_vecs[0:1, :]
        + points[:, 1:2] * wave_vecs[1:2, :]
        + points[:, 2:3] * wave_vecs[2:3, :]
    )


def mix_vectors(s_re, s_im, mix_pair, wave_filter, scale):
    a_re = (s_re * scale).astype(jnp.bfloat16)
    a_im = (s_im * scale).astype(jnp.bfloat16)
    real_real = jnp.dot(a_re, mix_pair[0], preferred_element_type=jnp.float32)
    imag_imag = jnp.dot(a_im, mix_pair[1], preferred_element_type=jnp.float32)
    real_imag = jnp.dot(a_re, mix_pair[1], preferred_element_type=jnp.float32)
    imag_real = jnp.dot(a_im, mix_pair[0], preferred_element_type=jnp.float32)
    y_re = (wave_filter * (real_real - imag_imag)).astype(jnp.bfloat16)
    y_im = (wave_filter * (real_imag + imag_real)).astype(jnp.bfloat16)
    return (y_re, y_im)


def wave_terms(points, wave_vecs, y_re, y_im, inv_scale):
    angles = phase_angles(points, wave_vecs)
    cos_part = jnp.cos(angles).astype(jnp.bfloat16)
    sin_part = jnp.sin(angles).astype(jnp.bfloat16)
    summed = jnp.dot(cos_part, y_re, preferred_element_type=jnp.float32) + jnp.dot(
        sin_part, y_im, preferred_element_type=jnp.float32
    )
    return summed * inv_scale


def structure_piece(carry, piece, positions, wave_vecs):
    count = piece.shape[0]
    block = 512
    dims = (((0,), (0,)), ((), ()))

    def one_block(block_id, totals):
        offset = (block_id * block).astype(jnp.int32)
        feat_block = lax.dynamic_slice_in_dim(piece, offset, block, 0)
        pos_block = lax.dynamic_slice_in_dim(positions, offset, block, 0)
        angles = phase_angles(pos_block, wave_vecs)
        cos_part = jnp.cos(angles).astype(jnp.bfloat16)
        sin_part = jnp.sin(angles).astype(jnp.bfloat16)
        new_re = totals[0] + lax.dot_general(
            cos_part, feat_block, dims, preferred_element_type=jnp.float32
        )
        new_im = totals[1] + lax.dot_general(
            sin_part, feat_block, dims, preferred_element_type=jnp.float32
        )
        return (new_re, new_im)

    return lax.fori_loop(0, count // block, one_block, carry)


def local(
    features,
    positions,
    wave_index,
    wave_filter,
    mix_pair,
    msg_weight,
    chan_width,
    pair_dist,
    neighbours,
    norm_gain,
    in_weight,
    out_weight,
):
    atom_dev = features.shape[0]
    channels = features.shape[1]
    groups = lax.axis_size("kgrp")
    total_atoms = atom_dev * groups * lax.axis_size("space")
    halo_width = atom_dev // 4
    projected = jnp.dot(features, msg_weight, preferred_element_type=jnp.float32).astype(
        jnp.bfloat16
    )
    extended = padded(projected, ((("space", "kgrp"), 0),), halo_width)
    nearby = jnp.take(extended, neighbours, axis=0)
    weights = jnp.exp(-pair_dist[:, :, None] / chan_width[None, None, :])
    message = jnp.sum(weights * nearby.astype(jnp.float32), axis=1)
    wave_vecs = wave_vectors(wave_index, total_atoms * slab_step)
    wave_count = wave_index.shape[0]
    zeros = jnp.zeros((wave_count, channels), jnp.float32)
    partial_sums = structure_piece(
        (zeros, zeros), lax.all_gather(features, "kgrp", axis=0, tiled=True), positions, wave_vecs
    )
    scale = 1.0 / math.sqrt(total_atoms)
    s_re, s_im = lax.psum((partial_sums[0], partial_sums[1]), "space")
    y_re, y_im = mix_vectors(s_re, s_im, mix_pair, wave_filter, scale)
    inv_scale = 1.0 / math.sqrt(wave_count * groups)
    block = 512
    stacked = positions.reshape(lax.axis_size("kgrp") * atom_dev // block, block, 3)
    terms = lax.map(
        lambda group_points: wave_terms(group_points, wave_vecs, y_re, y_im, inv_scale), stacked
    )
    ewald = lax.psum_scatter(
        terms.reshape(lax.axis_size("kgrp") * atom_dev, channels).astype(jnp.bfloat16),
        "kgrp",
        scatter_dimension=0,
        tiled=True,
    ).astype(jnp.float32)
    mixed = features.astype(jnp.float32) + message + ewald
    inverse = lax.rsqrt(jnp.mean(mixed * mixed, axis=1, keepdims=True) + 1e-06)
    normed = (mixed * inverse * norm_gain).astype(jnp.bfloat16)
    hidden = jax.nn.silu(jnp.dot(normed, in_weight, preferred_element_type=jnp.float32)).astype(
        jnp.bfloat16
    )
    return (mixed + jnp.dot(hidden, out_weight, preferred_element_type=jnp.float32)).astype(
        jnp.bfloat16
    )


def solution(mesh):
    placed = (
        P(("space", "kgrp"), None),
        P("space", None),
        P("kgrp", None),
        P("kgrp", None),
        P(),
        P(),
        P(),
        P(("space", "kgrp"), None),
        P(("space", "kgrp"), None),
        P(),
        P(),
        P(),
    )
    return jax.shard_map(
        local, mesh=mesh, in_specs=placed, out_specs=P(("space", "kgrp"), None), check_vma=False
    )
```

profile of v0, /device:TPU:1, one launch (start us, length us, event | category | flops | bytes accessed | tf_op | source)
XLA Modules:
  0.0 618.7 jit_solution(11040318629866521014)
XLA Ops:
  6.5 0.7 convert_element_type.65
  7.3 29.8 %all_gather.3 = bf16[1024,128]{1,0:T(8,128)(2,1)S(1)} all-gather(bf16[128,128]{1,0:T(8,128)(2,1)} %param.16), channel_id=1, replica_groups=mesh['space'=64,'kgrp'=8] {'kgrp'}, dimensions={0}, use_global_device_ids=true | all-gather | bytes 294912 | tf_op jit(solution)/shard_map/all_gather | solution.py:121
  37.1 24.7 %while.27 = (s32[]{:T(128)}, f32[768,128]{1,0:T(8,128)S(1)}, f32[768,128]{1,0:T(8,128)S(1)}, f32[1024,3]{0,1:T(4,128)}, f32[1,768]{1,0:T(1,128)S(1)}, /*index=5*...) while((s32[]{:T(128)}, f32[768,128]{1,0:T(8,128)S(1)}, ...), condition=%wide.region_2.3_spmd.clone, body=%wide.region_1.2_spmd.clone.sunk | while | flops 206438400 | bytes 1902846 | solution.py:88
  37.1 0.9 constant_dynamic-slice_fusion.2
  38.0 5.7 convolution_add_fusion.8
  43.8 5.7 convolution_add_fusion.7
  49.5 0.9 constant_dynamic-slice_fusion.2
  50.4 5.7 convolution_add_fusion.8
  56.1 5.7 convolution_add_fusion.7
  61.9 0.0 copy-start.7
  61.9 0.0 copy-start.10
  61.9 0.0 copy-start.11
  61.9 0.0 copy-start.8
  61.9 0.7 copy-done.4
  62.6 0.2 copy-done.5
  62.7 0.0 all-reduce.3.cloned.1.call-update
  62.8 0.2 reduce-scatter.2.cloned.1.call-start
  63.0 0.1 convolution_convert_fusion
  63.2 2.7 collective-permute-start
  65.9 12.5 %collective-permute-start.1 = (bf16[32,128]{1,0:T(8,128)(2,1)S(1)}, bf16[32,128]{1,0:T(8,128)(2,1)S(1)}, u32[]{:S(2)}, u32[]{:S(2)}) collective-permute-start(bf16[32,128]{1,0:T(8,128)(2,1)S(1)} %get-tuple-element.258), channel_id=1, source_target_pairs={{1,0},{2,1},{3,2},{4,3},{5,4},{6,5},{7,6},{8,7},{9,8},{10,9},{11,1... | collective-permute-start | bytes 24584 | tf_op jit(solution)/shard_map/ppermute | solution.py:21
  78.4 0.1 copy.17
  78.5 0.1 reshape.61
  78.6 419.4 %all-reduce.3.cloned.1.call-done = (f32[768,128]{1,0:T(8,128)}, f32[768,128]{1,0:T(8,128)}) async-done(((f32[768,128]{1,0:T(8,128)}, f32[768,128]{1,0:T(8,128)}), (f32[768,128]{1,0:T(8,128)}, f32[768,128]{1,0:T(8,128)})) %all-reduce.3.cloned.1.call-update) | async-done | bytes 786448 | tf_op jit(solution)/shard_map/psum | solution.py:124
  498.0 1.3 fusion.30
  499.3 0.0 copy-start.2
  499.3 0.2 fusion.31
  499.5 0.8 copy-done.2
  500.3 0.1 copy-done.3
  500.4 0.2 fusion.25
  500.6 0.0 copy-start.6
  500.6 0.2 fusion.26
  500.8 0.5 copy-done.6
  501.3 22.8 %while.26 = (s32[]{:T(128)}, bf16[2,512,128]{2,1,0:T(8,128)(2,1)S(1)}, f32[2,512,3]{1,2,0:T(4,128)S(1)}, f32[1,768]{1,0:T(1,128)S(1)}, f32[1,768]{1,0:T(1,128)S(...) while((s32[]{:T(128)}, ...), condition=%wide.region_6.7_spmd, body=%wide.region_5.6_spmd.sunk | while | flops 206176256 | bytes 1256569 | solution.py:129
  501.4 5.5 fusion.71
  506.9 5.8 fusion.72
  512.8 5.5 fusion.71
  518.3 5.8 fusion.72
  524.2 0.7 copy-done.9
  524.8 0.0 reduce-scatter.2.cloned.1.call-update
  524.9 0.1 copy.15
  525.0 0.1 copy.16
  525.2 0.0 copy-start.13
  525.2 6.2 %gather_fusion = bf16[2048,128]{1,0:T(8,128)(2,1)S(1)} fusion(bf16[192,128]{1,0:T(8,128)(2,1)S(1)} %pad_maximum_fusion, s32[2048]{0:T(1024)S(1)} %broadcast_clamp_fusion), kind=kCustom, calls=%fused_computation | custom fusion | bytes 1056768 | tf_op jit(solution)/shard_map/jit(_take)/gather | solution.py:114
  531.4 0.0 copy-start.14
  531.4 0.8 fusion.29
  532.2 76.9 %reduce-scatter.2.cloned.1.call-done = bf16[128,128]{1,0:T(8,128)(2,1)} async-done(((bf16[1024,128]{1,0:T(8,128)(2,1)}), bf16[128,128]{1,0:T(8,128)(2,1)}) %reduce-scatter.2.cloned.1.call-update) | async-done | bytes 32784 | tf_op jit(solution)/shard_map/reduce_scatter | solution.py:132
  609.1 0.9 multiply_reduce_fusion
  610.0 1.9 fusion.27
  (48 shorter events, 0.3 us)
Async XLA Ops:
  6.5 603.5 %copy-start = (bf16[512,128]{1,0:T(8,128)(2,1)S(1)}, bf16[512,128]{1,0:T(8,128)(2,1)}, u32[]{:S(2)}) copy-start(bf16[512,128]{1,0:T(8,128)(2,1)} %param.27) | copy-start | bytes 393220
  6.5 491.5 %all-reduce.3.cloned.1.call-start = ((), (), s32[]{:S(2)}) async-start(), calls=%async_computation.2 | async-start | bytes 1572864 | tf_op jit(solution)/shard_map/psum | solution.py:124
  61.8 0.7 copy-start.4
  61.8 0.9 copy-start.5
  61.9 1.1 copy-start.7
  61.9 1.1 copy-start.10
  61.9 16.5 %copy-start.11 = (s32[128,16]{0,1:T(8,128)S(1)}, s32[128,16]{0,1:T(8,128)}, u32[]{:S(2)}) copy-start(s32[128,16]{0,1:T(8,128)} %param.24) | copy-start | bytes 24580
  61.9 436.1 %copy-start.8 = (bf16[2,128,128]{2,1,0:T(8,128)(2,1)S(1)}, bf16[2,128,128]{2,1,0:T(8,128)(2,1)}, u32[]{:S(2)}) copy-start(bf16[2,128,128]{2,1,0:T(8,128)(2,1)} %param.20) | copy-start | bytes 196612
  62.8 546.4 %reduce-scatter.2.cloned.1.call-start = ((), (), s32[]{:S(2)}) async-start(), calls=%async_computation.1 | async-start | bytes 294912 | tf_op jit(solution)/shard_map/reduce_scatter | solution.py:132
  63.2 462.0 %collective-permute-start = (bf16[32,128]{1,0:T(8,128)(2,1)S(1)}, bf16[32,128]{1,0:T(8,128)(2,1)S(1)}, u32[]{:S(2)}, u32[]{:S(2)}) collective-permute-start(bf16[32,128]{1,0:T(8,128)(2,1)S(1)} %get-tuple-element.257), channel_id=1, source_target_pairs={{0,1},{1,2},{2,3},{3,4},{4,5},{5,6},{6,7},{7,8},{8,9},{9,10},{10,1... | collective-permute-start | bytes 24584 | tf_op jit(solution)/shard_map/ppermute | solution.py:20
  65.9 459.3 %collective-permute-start.1 = (bf16[32,128]{1,0:T(8,128)(2,1)S(1)}, bf16[32,128]{1,0:T(8,128)(2,1)S(1)}, u32[]{:S(2)}, u32[]{:S(2)}) collective-permute-start(bf16[32,128]{1,0:T(8,128)(2,1)S(1)} %get-tuple-element.258), channel_id=1, source_target_pairs={{1,0},{2,1},{3,2},{4,3},{5,4},{6,5},{7,6},{8,7},{9,8},{10,9},{11,1... | collective-permute-start | bytes 24584 | tf_op jit(solution)/shard_map/ppermute | solution.py:21
  498.0 1.3 copy-start.1
  499.3 1.0 copy-start.2
  499.3 1.1 copy-start.3
  500.6 0.7 copy-start.6
  501.3 23.5 %copy-start.12 = (f32[128,16]{0,1:T(8,128)S(1)}, f32[128,16]{0,1:T(8,128)}, u32[]{:S(2)}) copy-start(f32[128,16]{0,1:T(8,128)} %param.23) | copy-start | bytes 24580
  524.2 0.7 copy-start.9
  525.2 6.2 %copy-start.13 = (f32[128]{0:T(128)S(1)}, f32[128]{0:T(128)}, u32[]{:S(2)}) copy-start(f32[128]{0:T(128)} %param.22) | copy-start | bytes 1540
  531.4 78.6 %copy-start.14 = (bf16[128,512]{1,0:T(8,128)(2,1)S(1)}, bf16[128,512]{1,0:T(8,128)(2,1)}, u32[]{:S(2)}) copy-start(bf16[128,512]{1,0:T(8,128)(2,1)} %param.26) | copy-start | bytes 393220
  531.4 78.6 %copy-start.15 = (f32[128]{0:T(128)S(1)}, f32[128]{0:T(128)}, u32[]{:S(2)}) copy-start(f32[128]{0:T(128)} %param.25) | copy-start | bytes 1540
Sparse Core Ops, SparseCore 0:
  62.9 435.1 all-reduce.2
  525.0 84.0 reduce-scatter.1
where the time goes:
time: 620 us; the launch traced here: 619 us
  waiting for transfers between devices  496 us (80%)
  matrix products  49.2 us (8%)
  blocking collectives  29.8 us (5%)
  starting transfers between devices  15.4 us (2%)
  between operations  13.7 us (2%)
  local copies, waits for them, and re-layouts  11.4 us (2%)
    psum x1, waiting for transfers between devices, local(): s_re, s_im = lax.psum((partial_sums[0], partial_sums[1]), 'space')  419 us
    reduce_scatter x1, waiting for transfers between devices, local(): lax.psum_scatter(terms.reshape(lax.axis_size('kgrp') * atom_dev, channels...  76.9 us
    all_gather x1, blocking collectives, local(): lax.all_gather(features, 'kgrp', axis=0, tiled=True)  29.8 us
    ppermute x1, starting transfers between devices, padded(): after = lax.ppermute(first, axis, down)  12.5 us
  transfers between devices with their start and end apart: 4, of which 2 were waited for; matrix products, arithmetic and copies ran while one was open for 5% of the time, Pallas kernels for 0%

commit v1 on v0

v1 whole, which is shorter than its diff:
```python
import functools
import math

import jax
import jax.numpy as jnp
import numpy as np
from jax import lax
from jax.experimental import pallas as pl
from jax.experimental.pallas import tpu as pltpu
from jax.sharding import PartitionSpec as P

MESH = pl.DeviceIdType.MESH
BOX = 16.0
SLAB_STEP = 0.125
F = 128
WB = 12
TN = (((0,), (0,)), ((), ()))
NN = (((1,), (0,)), ((), ()))

def fit_poly():
    r = 0.5 * np.cos(np.pi * (np.arange(4001) + 0.5) / 4001 / 2)
    t = r * r
    cheb = np.polynomial.chebyshev
    sin_p = cheb.Chebyshev.fit(t, np.sin(np.pi * r) / r, 4, domain=[0.0, 0.25])
    cos_p = cheb.Chebyshev.fit(t, np.cos(np.pi * r), 5, domain=[0.0, 0.25])
    to = lambda p: tuple(float(v) for v in p.convert(kind=np.polynomial.Polynomial).coef)
    return to(sin_p), to(cos_p)


SIN_C, COS_C = fit_poly()


def cos_sin_turns(u):
    r = u - jnp.round(u)
    t = r * r
    s = jnp.full_like(t, SIN_C[-1])
    for coef in SIN_C[-2::-1]:
        s = s * t + coef
    s = s * r
    c = jnp.full_like(t, COS_C[-1])
    for coef in COS_C[-2::-1]:
        c = c * t + coef
    s2 = s + s
    return 1.0 - s2 * s, s2 * c


def split3(v):
    hi = v.astype(jnp.bfloat16)
    rest = v - hi.astype(jnp.float32)
    mid = rest.astype(jnp.bfloat16)
    low = (rest - mid.astype(jnp.float32)).astype(jnp.bfloat16)
    return hi, mid, low


def low_rows(shape):
    return lax.broadcasted_iota(jnp.int32, shape, len(shape) - 2) < 4


def to_blocks(re, im):
    pairs = re.shape[0] // (2 * WB)
    a = re.reshape(pairs, 3, 8, F)
    b = im.reshape(pairs, 3, 8, F)
    a0, a1, a2 = a[:, 0], a[:, 1], a[:, 2]
    b0, b1, b2 = b[:, 0], b[:, 1], b[:, 2]
    low = low_rows(a1.shape)
    x = jnp.where(low, a1, pltpu.roll(b1, 4, 1))
    y = jnp.where(low, pltpu.roll(a1, 4, 1), b1)
    first = jnp.stack([a0, b0, x], axis=1)
    second = jnp.stack([a2, b2, y], axis=1)
    return jnp.stack([first, second], axis=1).reshape(2 * pairs, 3, 8, F)


def from_blocks(v):
    pairs = v.shape[0] // 2
    v = v.reshape(pairs, 2, 3, 8, F)
    x, y = v[:, 0, 2], v[:, 1, 2]
    low = low_rows(x.shape)
    a1 = jnp.where(low, x, pltpu.roll(y, 4, 1))
    b1 = jnp.where(low, pltpu.roll(x, 4, 1), y)
    re = jnp.stack([v[:, 0, 0], a1, v[:, 1, 0]], axis=1).reshape(pairs * 24, F)
    im = jnp.stack([v[:, 0, 1], b1, v[:, 1, 1]], axis=1).reshape(pairs * 24, F)
    return re, im


def far_first(n):
    return sorted(range(1, n), key=lambda o: -min(o, n - o))


def kernel(
    zs, gs, feat, pos, wave, filt, mix, msgw, width, dist, nbr, gain, inw, outw, out,
    fall, halo, ut, ptc, pts, pc, ps, acc, sc_buf, rc_buf, sy_buf, ry_buf, sz_buf, rz_buf,
    ysrc, yall, yre, yim, es, er, msg_t, own_e,
    ag_s, ag_r, ha_s, ha_r, c_s, c_r, y_s, y_r, z_s, z_r, zb_s, zb_r, yb_s, yb_r, cb_s, cb_r, e_s, e_r,
):
    f32, bf16 = jnp.float32, jnp.bfloat16
    dot = functools.partial(lax.dot_general, preferred_element_type=f32)
    me_s, me_g = lax.axis_index("space"), lax.axis_index("kgrp")
    z, yl, c = me_s // 4, lax.rem(me_s // 2, 2), lax.rem(me_s, 2)
    n_dev = 4 * zs * gs
    flat = me_s * gs + me_g
    up, down = lax.rem(flat + 1, n_dev), lax.rem(flat + n_dev - 1, n_dev)
    up = (up // gs, lax.rem(up, gs))
    down = (down // gs, lax.rem(down, gs))
    group = [(me_s, lax.rem(me_g + o, gs)) for o in range(gs)]
    core = (z * 4 + yl * 2 + 1 - c, me_g)
    ypeer = (z * 4 + (1 - yl) * 2 + c, me_g)
    ring = [(lax.rem(z + o, zs) * 4 + yl * 2 + c, me_g) for o in range(zs)]
    atoms = feat.shape[0]
    kw = wave.shape[1]
    half, quarter = 2 * zs, zs

    def remote(src, dst, send, recv, device):
        return pltpu.make_async_remote_copy(
            src_ref=src, dst_ref=dst, send_sem=send, recv_sem=recv, device_id=device, device_id_type=MESH
        )

    barrier = pltpu.get_barrier_semaphore()
    peers = group[1:] + [up, down, core, ypeer] + ring[1:]
    for device in peers:
        pl.semaphore_signal(barrier, inc=1, device_id=device, device_id_type=MESH)

    scales = lax.broadcasted_iota(jnp.int32, pos.shape, 0)
    scales = jnp.where(scales < 2, 1.0 / BOX, 1.0 / (n_dev * atoms * SLAB_STEP)).astype(f32)
    pieces = split3(pos[...] * scales)
    counts = wave[...].astype(f32).astype(bf16)

    def trig(lhs_rhs, cos_ref, sin_ref):
        total = None
        for lhs, rhs in lhs_rhs:
            part = dot(lhs, rhs, TN)
            total = part if total is None else total + part
        rows, cols = total.shape
        ut[0:rows, 0:cols] = total

        def body(i, carry):
            at = pl.ds(pl.multiple_of(i * 16, 16), 16)
            cos_v, sin_v = cos_sin_turns(ut[at, 0:cols])
            cos_ref[at, :] = cos_v.astype(bf16)
            sin_ref[at, :] = sin_v.astype(bf16)
            return carry

        lax.fori_loop(0, rows // 16, body, 0)

    trig([(counts, p) for p in pieces], ptc, pts)

    pl.semaphore_wait(barrier, len(peers))

    gather = []
    for o in far_first(gs):
        copy = remote(feat, fall.at[me_g], ag_s.at[o], ag_r.at[o], group[o])
        copy.start()
        gather.append((o, copy))
    edge = atoms // 4
    halo_up = remote(feat.at[pl.ds(atoms - edge, edge)], halo.at[0], ha_s.at[0], ha_r.at[0], up)
    halo_down = remote(feat.at[pl.ds(0, edge)], halo.at[1], ha_s.at[1], ha_r.at[1], down)
    halo_up.start()
    halo_down.start()
    fall[pl.ds(me_g, 1)] = feat[...][None]

    for o, copy in gather:
        copy.wait()

    feats = fall[...].reshape(gs * atoms, F)

    def structure(half_index):
        at = pl.ds(pl.multiple_of(half_index * (kw // 2), 8), kw // 2)
        return to_blocks(dot(ptc[at, :], feats, NN), dot(pts[at, :], feats, NN))

    sc_buf[...] = structure(1 - c).astype(bf16)
    copy_c = remote(sc_buf, rc_buf, c_s, c_r, core)
    copy_c.start()
    acc[...] = structure(c)
    copy_c.wait()
    theirs = pl.ds((1 - yl) * quarter, quarter)
    mine = pl.ds(yl * quarter, quarter)
    sy_buf[...] = (acc[theirs] + rc_buf[theirs].astype(f32)).astype(bf16)
    copy_y = remote(sy_buf, ry_buf, y_s, y_r, ypeer)
    copy_y.start()
    acc[mine] = acc[mine] + rc_buf[mine].astype(f32)
    copy_y.wait()
    acc[mine] = acc[mine] + ry_buf[...].astype(f32)
    sz_buf[...] = acc[mine].astype(bf16)
    ring_copies = []
    for o in far_first(zs):
        copy = remote(sz_buf.at[lax.rem(z + o, zs)], rz_buf.at[z], z_s.at[o], z_r.at[o], ring[o])
        copy.start()
        ring_copies.append((o, copy))

    trig([(p, counts) for p in pieces], pc, ps)

    halo_up.wait()
    halo_down.wait()
    weight = msgw[...]
    ext = jnp.concatenate(
        [
            dot(halo[0], weight, NN),
            dot(feat[...], weight, NN),
            dot(halo[1], weight, NN),
            jnp.zeros((edge * 2, F), f32),
        ],
        axis=0,
    )
    ext_t = ext.T.astype(bf16)
    inv_width = (1.0 / jnp.broadcast_to(width[...], (F, F))).T
    row_ids = lax.broadcasted_iota(jnp.int32, (2 * atoms, atoms), 0)
    message = jnp.zeros((F, atoms), f32)
    for j in range(nbr.shape[0]):
        hot = jnp.where(row_ids == nbr[j : j + 1, :], 1.0, 0.0).astype(bf16)
        near = dot(ext_t, hot, NN)
        message = message + jnp.exp(-(dist[j : j + 1, :] * inv_width)) * near
    msg_t[...] = message.T

    own = yl * quarter + z
    total = acc[pl.ds(own, 1)][0]
    for o, copy in ring_copies:
        copy.wait()
        total = total + rz_buf[pl.ds(lax.rem(z + zs - o, zs), 1)][0].astype(f32)

    a = (total * (1.0 / math.sqrt(n_dev * atoms))).reshape(24, F).astype(bf16)
    r0 = dot(a, mix[0], NN).reshape(3, 8, F)
    r1 = dot(a, mix[1], NN).reshape(3, 8, F)
    block = c * half + own
    pair = block // 2
    odd = lax.rem(block, 2) == 1
    fil = filt[pl.ds(pl.multiple_of(pair * 24, 8), 24), :].reshape(3, 8, F)
    low = low_rows((8, F))
    swapped = pltpu.roll(fil[1], 4, 0)
    f_main = jnp.where(odd, fil[2], fil[0])
    f_mixed = jnp.where(jnp.logical_xor(low, odd), fil[1], swapped)
    r1_swapped = pltpu.roll(r1[2], 4, 0)
    y_val = jnp.stack(
        [
            f_main * (r0[0] - r1[1]),
            f_main * (r1[0] + r0[1]),
            f_mixed * jnp.where(low, r0[2] - r1_swapped, r0[2] + r1_swapped),
        ],
        axis=0,
    ).astype(bf16)
    ysrc[...] = y_val
    back = []
    for o in far_first(zs):
        copy = remote(ysrc, yall.at[block], zb_s.at[o], zb_r.at[o], ring[o])
        copy.start()
        back.append(copy)
    yall[pl.ds(block, 1)] = y_val[None]
    for copy in back:
        copy.wait()
    mine_y = yall.at[pl.ds(c * half + yl * quarter, quarter)]
    copy_yb = remote(mine_y, mine_y, yb_s, yb_r, ypeer)
    copy_yb.start()
    copy_yb.wait()
    mine_c = yall.at[pl.ds(c * half, half)]
    copy_cb = remote(mine_c, mine_c, cb_s, cb_r, core)
    copy_cb.start()
    copy_cb.wait()

    re, im = from_blocks(yall[...].astype(f32))
    yre[...] = re.astype(bf16)
    yim[...] = im.astype(bf16)
    inv_scale = 1.0 / math.sqrt(kw * gs)

    def terms(g):
        at = pl.ds(pl.multiple_of(g * atoms, atoms), atoms)
        return (dot(pc[at, :], yre[...], NN) + dot(ps[at, :], yim[...], NN)) * inv_scale

    exchange = []
    for o in far_first(gs):
        es[o] = terms(lax.rem(me_g + o, gs)).astype(bf16)
        copy = remote(es.at[o], er.at[o], e_s.at[o], e_r.at[o], group[o])
        copy.start()
        exchange.append((o, copy))
    ewald = terms(me_g)
    for o, copy in exchange:
        copy.wait()
        ewald = ewald + er[o].astype(f32)

    mixed = feat[...].astype(f32) + msg_t[...] + ewald
    inverse = lax.rsqrt(jnp.mean(mixed * mixed, axis=1, keepdims=True) + 1e-06)
    normed = (mixed * inverse * gain[...]).astype(bf16)
    pre = dot(normed, inw[...], NN)
    hidden = (pre * (1.0 / (1.0 + jnp.exp(-pre)))).astype(bf16)
    out[...] = (mixed + dot(hidden, outw[...], NN)).astype(bf16)


def solution(mesh):
    zs, gs = mesh.shape["space"] // 4, mesh.shape["kgrp"]

    def local(features, positions, wave_index, wave_filter, mix_pair, msg_weight, chan_width, pair_dist,
              neighbours, norm_gain, in_weight, out_weight):
        atoms = features.shape[0]
        dom = gs * atoms
        kw = wave_index.shape[0]
        f32, bf16 = jnp.float32, jnp.bfloat16
        blk = (3, 8, F)
        nb, nh, nq = 4 * zs, 2 * zs, zs
        big = max(kw, dom)
        vm = pltpu.VMEM
        dma = pltpu.SemaphoreType.DMA
        scratch = [
            vm((gs, atoms, F), bf16),
            vm((2, atoms // 4, F), bf16),
            vm((big, big), f32),
            vm((kw, dom), bf16),
            vm((kw, dom), bf16),
            vm((dom, kw), bf16),
            vm((dom, kw), bf16),
            vm((nh, *blk), f32),
            vm((nh, *blk), bf16),
            vm((nh, *blk), bf16),
            vm((nq, *blk), bf16),
            vm((nq, *blk), bf16),
            vm((nq, *blk), bf16),
            vm((nq, *blk), bf16),
            vm(blk, bf16),
            vm((nb, *blk), bf16),
            vm((kw, F), bf16),
            vm((kw, F), bf16),
            vm((gs, atoms, F), bf16),
            vm((gs, atoms, F), bf16),
            vm((atoms, F), f32),
            vm((atoms, F), f32),
            dma((gs,)), dma((gs,)), dma((2,)), dma((2,)),
            dma, dma, dma, dma,
            dma((zs,)), dma((zs,)), dma((zs,)), dma((zs,)),
            dma, dma, dma, dma,
            dma((gs,)), dma((gs,)),
        ]
        return pl.pallas_call(
            functools.partial(kernel, zs, gs),
            out_shape=jax.ShapeDtypeStruct((atoms, F), bf16),
            in_specs=[pl.BlockSpec(memory_space=pltpu.VMEM)] * 12,
            out_specs=pl.BlockSpec(memory_space=pltpu.VMEM),
            scratch_shapes=scratch,
            compiler_params=pltpu.CompilerParams(
                collective_id=0, has_side_effects=True, vmem_limit_bytes=60 * 1024 * 1024
            ),
        )(
            features, positions.T, wave_index.T, wave_filter, mix_pair, msg_weight,
            chan_width.reshape(1, F), pair_dist.T, neighbours.T, norm_gain.reshape(1, F), in_weight, out_weight,
        )

    placed = (
        P(("space", "kgrp"), None), P("space", None), P("kgrp", None), P("kgrp", None), P(), P(), P(),
        P(("space", "kgrp"), None), P(("space", "kgrp"), None), P(), P(), P(),
    )
    return jax.shard_map(
        local, mesh=mesh, in_specs=placed, out_specs=P(("space", "kgrp"), None), check_vma=False
    )
```

time: 620 us -> 60.2 us (0.10)
  waiting for transfers between devices: 496 us -> 0 us
  Pallas kernels: 0 us -> 58.5 us
  matrix products: 49.2 us -> 0 us
  blocking collectives: 29.8 us -> 0 us
  starting transfers between devices: 15.4 us -> 0 us
  between operations: 13.7 us -> 0.01 us
  local copies, waits for them, and re-layouts: 11.4 us -> 1.38 us
    psum x1 -> x0, waiting for transfers between devices: 419 us -> none  [local(): s_re, s_im = lax.psum((partial_sums[0], partial_sums[1]), 'space')]
    reduce_scatter x1 -> x0, waiting for transfers between devices: 76.9 us -> none  [local(): lax.psum_scatter(terms.reshape(lax.axis_size('kgrp') * atom_dev, channels...]
    pallas_call x0 -> x1, Pallas kernels: none -> 58.5 us  [local(): pl.pallas_call(functools.partial(kernel, zs, gs), out_shape=jax.ShapeDtyp...]
    dot_general x14 -> x0, matrix products: 49.2 us -> none  [the longest x2 11.7 us: wave_terms(): jnp.dot(sin_part, y_im, preferred_element_type=jnp.float32)]
    all_gather x1 -> x0, blocking collectives: 29.8 us -> none  [local(): lax.all_gather(features, 'kgrp', axis=0, tiled=True)]
    ppermute x2 -> x0, starting transfers between devices: 15.2 us -> none  [the longest x1 12.5 us: padded(): after = lax.ppermute(first, axis, down)]
  transfers between devices with their start and end apart: 4 -> 0, of which waited for: 2 -> 0; matrix products, arithmetic and copies ran while one was open for 5% -> 0% of each run, Pallas kernels for 0% -> 0%
where the time goes in v1:
time: 60.2 us; the launch traced here: 59.9 us
  Pallas kernels  58.5 us (97%)
  local copies, waits for them, and re-layouts  1.38 us (2%)
    pallas_call x1, Pallas kernels, local(): pl.pallas_call(functools.partial(kernel, zs, gs), out_shape=jax.ShapeDtyp...  58.5 us
    unnamed x1, local copies, waits for them, and re-layouts  1.38 us

profile of v1, /device:TPU:1, one launch (start us, length us, event | category | flops | bytes accessed | tf_op | source)
XLA Modules:
  0.0 59.9 jit_solution(10857190393458342175)
XLA Ops:
  0.0 58.5 %shard_map.118 = bf16[128,128]{1,0:T(8,128)(2,1)} custom-call(bf16[128,128]{1,0:T(8,128)(2,1)} %feat.1, f32[3,1024]{1,0:T(4,128)} %bitcast.6, s32[3,768]{1,0:T(4,128)} %bitcast.7, f32[768,128]{1,0:T(8,128)} %filt.1, bf16[2,128,128]{2,1,0:T(8,128)(2,1)} %mix.1, bf16[128,128]{1,0:T(8,128)(2,1)} %msgw.1, f32[1,128]{1,0:T(1,128)} %bitcast.10, ...), custom_call_target="tpu_custom_call" | custom-call | tf_op jit(solution)/shard_map/pallas_call | solution.py:328
  58.5 1.4 %copy.14 = bf16[128,128]{1,0:T(8,128)(2,1)} copy(bf16[128,128]{1,0:T(8,128)(2,1)} %shard_map.118) | data formatting | bytes 65536

commit v2 on v1

--- a/solution.py
+++ b/solution.py
@@ -86,11 +86,15 @@
     return sorted(range(1, n), key=lambda o: -min(o, n - o))
 
 
+def slot_of(o, n):
+    return 0 if o == 0 else 2 * o - 1 if o <= n // 2 else 2 * (n - o)
+
+
 def kernel(
     zs, gs, feat, pos, wave, filt, mix, msgw, width, dist, nbr, gain, inw, outw, out,
-    fall, halo, ut, ptc, pts, pc, ps, acc, sc_buf, rc_buf, sy_buf, ry_buf, sz_buf, rz_buf,
-    ysrc, yall, yre, yim, es, er, msg_t, own_e,
-    ag_s, ag_r, ha_s, ha_r, c_s, c_r, y_s, y_r, z_s, z_r, zb_s, zb_r, yb_s, yb_r, cb_s, cb_r, e_s, e_r,
+    fall, halo, ut, ptc, pts, pc, ps, stage, acc, sc_buf, rc_buf, sy_buf, ry_buf, sz_buf, rz_buf,
+    ysrc, yall, yre, yim, es, er, msg_t,
+    know, ag_s, ag_r, ha_s, ha_r, c_s, c_r, y_s, y_r, z_s, z_r, zb_s, zb_r, yb_s, yb_r, cb_s, cb_r, e_s, e_r,
 ):
     f32, bf16 = jnp.float32, jnp.bfloat16
     dot = functools.partial(lax.dot_general, preferred_element_type=f32)
@@ -104,33 +108,69 @@
     group = [(me_s, lax.rem(me_g + o, gs)) for o in range(gs)]
     core = (z * 4 + yl * 2 + 1 - c, me_g)
     ypeer = (z * 4 + (1 - yl) * 2 + c, me_g)
-    ring = [(lax.rem(z + o, zs) * 4 + yl * 2 + c, me_g) for o in range(zs)]
+    ring_z = [lax.rem(z + o, zs) for o in range(zs)]
+    ring = [(at * 4 + yl * 2 + c, me_g) for at in ring_z]
+    offset_of = sorted(range(zs), key=lambda o: slot_of(o, zs))
     atoms = feat.shape[0]
     kw = wave.shape[1]
-    half, quarter = 2 * zs, zs
+    rows = kw // 4
 
     def remote(src, dst, send, recv, device):
         return pltpu.make_async_remote_copy(
             src_ref=src, dst_ref=dst, send_sem=send, recv_sem=recv, device_id=device, device_id_type=MESH
         )
 
+    def signal(sem, device):
+        pl.semaphore_signal(sem, inc=1, device_id=device, device_id_type=MESH)
+
     barrier = pltpu.get_barrier_semaphore()
-    peers = group[1:] + [up, down, core, ypeer] + ring[1:]
+    peers = group[1:] + [up, down, core, ypeer, ring[1], ring[zs - 1]]
     for device in peers:
-        pl.semaphore_signal(barrier, inc=1, device_id=device, device_id_type=MESH)
+        signal(barrier, device)
 
     scales = lax.broadcasted_iota(jnp.int32, pos.shape, 0)
     scales = jnp.where(scales < 2, 1.0 / BOX, 1.0 / (n_dev * atoms * SLAB_STEP)).astype(f32)
     pieces = split3(pos[...] * scales)
     counts = wave[...].astype(f32).astype(bf16)
+
+    pl.semaphore_wait(barrier, len(peers))
+
+    gather = []
+    for o in far_first(gs):
+        copy = remote(feat, fall.at[me_g], ag_s.at[o], ag_r.at[o], group[o])
+        copy.start()
+        gather.append(copy)
+    edge = atoms // 4
+    halo_up = remote(feat.at[pl.ds(atoms - edge, edge)], halo.at[0], ha_s.at[0], ha_r.at[0], up)
+    halo_down = remote(feat.at[pl.ds(0, edge)], halo.at[1], ha_s.at[1], ha_r.at[1], down)
+    halo_up.start()
+    halo_down.start()
+    fall[pl.ds(me_g, 1)] = feat[...][None]
+
+    steps = []
+    reach = 1
+    while reach < zs // 2:
+        steps.append(reach)
+        reach *= 2
+
+    def tell(i):
+        if i < len(steps):
+            signal(know.at[i], ring[steps[i]])
+            signal(know.at[i], ring[zs - steps[i]])
+
+    def hear(i):
+        if i < len(steps):
+            pl.semaphore_wait(know.at[i], 2)
+
+    tell(0)
 
     def trig(lhs_rhs, cos_ref, sin_ref):
         total = None
         for lhs, rhs in lhs_rhs:
             part = dot(lhs, rhs, TN)
             total = part if total is None else total + part
-        rows, cols = total.shape
-        ut[0:rows, 0:cols] = total
+        n, cols = total.shape
+        ut[0:n, 0:cols] = total
 
         def body(i, carry):
             at = pl.ds(pl.multiple_of(i * 16, 16), 16)
@@ -139,54 +179,99 @@
             sin_ref[at, :] = sin_v.astype(bf16)
             return carry
 
-        lax.fori_loop(0, rows // 16, body, 0)
+        lax.fori_loop(0, n // 16, body, 0)
 
     trig([(counts, p) for p in pieces], ptc, pts)
-
-    pl.semaphore_wait(barrier, len(peers))
-
-    gather = []
-    for o in far_first(gs):
-        copy = remote(feat, fall.at[me_g], ag_s.at[o], ag_r.at[o], group[o])
-        copy.start()
-        gather.append((o, copy))
-    edge = atoms // 4
-    halo_up = remote(feat.at[pl.ds(atoms - edge, edge)], halo.at[0], ha_s.at[0], ha_r.at[0], up)
-    halo_down = remote(feat.at[pl.ds(0, edge)], halo.at[1], ha_s.at[1], ha_r.at[1], down)
-    halo_up.start()
-    halo_down.start()
-    fall[pl.ds(me_g, 1)] = feat[...][None]
-
-    for o, copy in gather:
+    hear(0)
+    tell(1)
+
+    for copy in gather:
         copy.wait()
+    hear(1)
+    tell(2)
 
     feats = fall[...].reshape(gs * atoms, F)
 
-    def structure(half_index):
-        at = pl.ds(pl.multiple_of(half_index * (kw // 2), 8), kw // 2)
-        return to_blocks(dot(ptc[at, :], feats, NN), dot(pts[at, :], feats, NN))
-
-    sc_buf[...] = structure(1 - c).astype(bf16)
-    copy_c = remote(sc_buf, rc_buf, c_s, c_r, core)
-    copy_c.start()
-    acc[...] = structure(c)
-    copy_c.wait()
-    theirs = pl.ds((1 - yl) * quarter, quarter)
-    mine = pl.ds(yl * quarter, quarter)
-    sy_buf[...] = (acc[theirs] + rc_buf[theirs].astype(f32)).astype(bf16)
-    copy_y = remote(sy_buf, ry_buf, y_s, y_r, ypeer)
-    copy_y.start()
-    acc[mine] = acc[mine] + rc_buf[mine].astype(f32)
-    copy_y.wait()
-    acc[mine] = acc[mine] + ry_buf[...].astype(f32)
-    sz_buf[...] = acc[mine].astype(bf16)
+    def structure(core_at, y_at):
+        at = pl.ds(pl.multiple_of((core_at * 2 + y_at) * rows, 8), rows)
+        stage[...] = to_blocks(dot(ptc[at, :], feats, NN), dot(pts[at, :], feats, NN))
+        return [stage[pl.ds(ring_z[o], 1)][0] for o in offset_of]
+
+    core_copies = []
+    for i, y_at in enumerate((1 - yl, yl)):
+        for s, v in enumerate(structure(1 - c, y_at)):
+            sc_buf[i, s] = v.astype(bf16)
+        copy = remote(sc_buf.at[i], rc_buf.at[i], c_s.at[i], c_r.at[i], core)
+        copy.start()
+        core_copies.append(copy)
+    cut = zs // 2
+    parts = (pl.ds(cut, zs - cut), pl.ds(0, cut))
+    mine = structure(c, 1 - yl)
+    core_copies[0].wait()
+    y_copies = []
+    for i, (lo, hi) in enumerate(((cut, zs), (0, cut))):
+        for s in range(lo, hi):
+            sy_buf[s] = (mine[s] + rc_buf[0, s].astype(f32)).astype(bf16)
+        copy = remote(sy_buf.at[parts[i]], ry_buf.at[parts[i]], y_s.at[i], y_r.at[i], ypeer)
+        copy.start()
+        y_copies.append(copy)
+    mine = structure(c, yl)
+    core_copies[1].wait()
+    for s in range(zs):
+        acc[s] = mine[s] + rc_buf[1, s].astype(f32)
+    hear(2)
     ring_copies = []
+    for i, (lo, hi) in enumerate(((cut, zs), (0, cut))):
+        y_copies[i].wait()
+        for s in range(hi - 1, lo - 1, -1):
+            total = acc[s] + ry_buf[s].astype(f32)
+            if s == 0:
+                acc[0] = total
+                continue
+            sz_buf[s] = total.astype(bf16)
+            o = offset_of[s]
+            back_slot = slot_of(zs - o, zs)
+            copy = remote(sz_buf.at[s], rz_buf.at[back_slot], z_s.at[s], z_r.at[back_slot], ring[o])
+            copy.start()
+            ring_copies.append(copy)
+
+    trig([(p, counts) for p in pieces], pc, ps)
+
+    total = acc[0]
+    for copy in ring_copies:
+        copy.wait()
+    for s in range(1, zs):
+        total = total + rz_buf[s].astype(f32)
+
+    a = (total * (1.0 / math.sqrt(n_dev * atoms))).reshape(24, F).astype(bf16)
+    r0 = dot(a, mix[0], NN).reshape(3, 8, F)
+    r1 = dot(a, mix[1], NN).reshape(3, 8, F)
+    odd = lax.rem(z, 2) == 1
+    pair = ((c * 2 + yl) * zs + z) // 2
+    fil = filt[pl.ds(pl.multiple_of(pair * 24, 8), 24), :].reshape(3, 8, F)
+    low = low_rows((8, F))
+    swapped = pltpu.roll(fil[1], 4, 0)
+    f_main = jnp.where(odd, fil[2], fil[0])
+    f_mixed = jnp.where(jnp.logical_xor(low, odd), fil[1], swapped)
+    r1_swapped = pltpu.roll(r1[2], 4, 0)
+    y_val = jnp.stack(
+        [
+            f_main * (r0[0] - r1[1]),
+            f_main * (r1[0] + r0[1]),
+            f_mixed * jnp.where(low, r0[2] - r1_swapped, r0[2] + r1_swapped),
+        ],
+        axis=0,
+    ).astype(bf16)
+    ysrc[...] = y_val
+    here = c * 2 + yl
+    beside = c * 2 + 1 - yl
+    back = {}
     for o in far_first(zs):
-        copy = remote(sz_buf.at[lax.rem(z + o, zs)], rz_buf.at[z], z_s.at[o], z_r.at[o], ring[o])
-        copy.start()
-        ring_copies.append((o, copy))
-
-    trig([(p, counts) for p in pieces], pc, ps)
+        s = slot_of(zs - o, zs)
+        copy = remote(ysrc, yall.at[here, s], zb_s.at[s], zb_r.at[s], ring[o])
+        copy.start()
+        back[s] = copy
+    yall[pl.ds(here, 1), 0] = y_val[None]
 
     halo_up.wait()
     halo_down.wait()
@@ -210,53 +295,42 @@
         message = message + jnp.exp(-(dist[j : j + 1, :] * inv_width)) * near
     msg_t[...] = message.T
 
-    own = yl * quarter + z
-    total = acc[pl.ds(own, 1)][0]
-    for o, copy in ring_copies:
+    if zs == 16:
+        cuts = (0, 5, 9, 13, 16)
+    else:
+        cuts = (0, zs // 2, zs)
+    y_back, core_back = [], []
+    for i in range(len(cuts) - 1):
+        lo, hi = cuts[i], cuts[i + 1]
+        for s in range(max(lo, 1), hi):
+            back[s].wait()
+        here_part = yall.at[here, pl.ds(lo, hi - lo)]
+        copy = remote(here_part, here_part, yb_s.at[i], yb_r.at[i], ypeer)
+        copy.start()
+        y_back.append(copy)
+        copy = remote(here_part, here_part, cb_s.at[i], cb_r.at[i], core)
+        copy.start()
+        core_back.append(copy)
+        beside_part = yall.at[beside, pl.ds(lo, hi - lo)]
+        copy = remote(beside_part, beside_part, cb_s.at[4 + i], cb_r.at[4 + i], core)
+        core_back.append(copy)
+        if i > 0:
+            y_back[i - 1].wait()
+            core_back[2 * i - 1].start()
+    y_back[-1].wait()
+    core_back[-1].start()
+    for copy in core_back:
         copy.wait()
-        total = total + rz_buf[pl.ds(lax.rem(z + zs - o, zs), 1)][0].astype(f32)
-
-    a = (total * (1.0 / math.sqrt(n_dev * atoms))).reshape(24, F).astype(bf16)
-    r0 = dot(a, mix[0], NN).reshape(3, 8, F)
-    r1 = dot(a, mix[1], NN).reshape(3, 8, F)
-    block = c * half + own
-    pair = block // 2
-    odd = lax.rem(block, 2) == 1
-    fil = filt[pl.ds(pl.multiple_of(pair * 24, 8), 24), :].reshape(3, 8, F)
-    low = low_rows((8, F))
-    swapped = pltpu.roll(fil[1], 4, 0)
-    f_main = jnp.where(odd, fil[2], fil[0])
-    f_mixed = jnp.where(jnp.logical_xor(low, odd), fil[1], swapped)
-    r1_swapped = pltpu.roll(r1[2], 4, 0)
-    y_val = jnp.stack(
-        [
-            f_main * (r0[0] - r1[1]),
-            f_main * (r1[0] + r0[1]),
-            f_mixed * jnp.where(low, r0[2] - r1_swapped, r0[2] + r1_swapped),
-        ],
-        axis=0,
-    ).astype(bf16)
-    ysrc[...] = y_val
-    back = []
-    for o in far_first(zs):
-        copy = remote(ysrc, yall.at[block], zb_s.at[o], zb_r.at[o], ring[o])
-        copy.start()
-        back.append(copy)
-    yall[pl.ds(block, 1)] = y_val[None]
-    for copy in back:
-        copy.wait()
-    mine_y = yall.at[pl.ds(c * half + yl * quarter, quarter)]
-    copy_yb = remote(mine_y, mine_y, yb_s, yb_r, ypeer)
-    copy_yb.start()
-    copy_yb.wait()
-    mine_c = yall.at[pl.ds(c * half, half)]
-    copy_cb = remote(mine_c, mine_c, cb_s, cb_r, core)
-    copy_cb.start()
-    copy_cb.wait()
-
-    re, im = from_blocks(yall[...].astype(f32))
-    yre[...] = re.astype(bf16)
-    yim[...] = im.astype(bf16)
+
+    slots = []
+    for t in range(zs):
+        o = lax.rem(t - z + zs, zs)
+        slots.append(jnp.where(o <= zs // 2, jnp.maximum(2 * o - 1, 0), 2 * (zs - o)))
+    for q in range(4):
+        blocks = [yall[q, pl.ds(slots[t], 1)] for t in range(zs)]
+        re, im = from_blocks(jnp.concatenate(blocks, axis=0).astype(f32))
+        yre[q * rows : (q + 1) * rows, :] = re.astype(bf16)
+        yim[q * rows : (q + 1) * rows, :] = im.astype(bf16)
     inv_scale = 1.0 / math.sqrt(kw * gs)
 
     def terms(g):
@@ -292,7 +366,6 @@
         kw = wave_index.shape[0]
         f32, bf16 = jnp.float32, jnp.bfloat16
         blk = (3, 8, F)
-        nb, nh, nq = 4 * zs, 2 * zs, zs
         big = max(kw, dom)
         vm = pltpu.VMEM
         dma = pltpu.SemaphoreType.DMA
@@ -304,25 +377,26 @@
             vm((kw, dom), bf16),
             vm((dom, kw), bf16),
             vm((dom, kw), bf16),
-            vm((nh, *blk), f32),
-            vm((nh, *blk), bf16),
-            vm((nh, *blk), bf16),
-            vm((nq, *blk), bf16),
-            vm((nq, *blk), bf16),
-            vm((nq, *blk), bf16),
-            vm((nq, *blk), bf16),
+            vm((zs, *blk), f32),
+            vm((zs, *blk), f32),
+            vm((2, zs, *blk), bf16),
+            vm((2, zs, *blk), bf16),
+            vm((zs, *blk), bf16),
+            vm((zs, *blk), bf16),
+            vm((zs, *blk), bf16),
+            vm((zs, *blk), bf16),
             vm(blk, bf16),
-            vm((nb, *blk), bf16),
+            vm((4, zs, *blk), bf16),
             vm((kw, F), bf16),
             vm((kw, F), bf16),
             vm((gs, atoms, F), bf16),
             vm((gs, atoms, F), bf16),
             vm((atoms, F), f32),
-            vm((atoms, F), f32),
+            pltpu.SemaphoreType.REGULAR((4,)),
             dma((gs,)), dma((gs,)), dma((2,)), dma((2,)),
-            dma, dma, dma, dma,
+            dma((2,)), dma((2,)), dma((2,)), dma((2,)),
             dma((zs,)), dma((zs,)), dma((zs,)), dma((zs,)),
-            dma, dma, dma, dma,
+            dma((4,)), dma((4,)), dma((8,)), dma((8,)),
             dma((gs,)), dma((gs,)),
         ]
         return pl.pallas_call(

time: 60.2 us -> 60.5 us (level)
  no operation moved by 1% of the time
where the time goes in v2:
time: 60.5 us; the launch traced here: 60.3 us
  Pallas kernels  58.9 us (97%)
  local copies, waits for them, and re-layouts  1.38 us (2%)
    pallas_call x1, Pallas kernels, local(): pl.pallas_call(functools.partial(kernel, zs, gs), out_shape=jax.ShapeDtyp...  58.9 us
    unnamed x1, local copies, waits for them, and re-layouts  1.38 us

profile of v2, /device:TPU:1, one launch (start us, length us, event | category | flops | bytes accessed | tf_op | source)
XLA Modules:
  0.0 60.3 jit_solution(17047411504657229841)
XLA Ops:
  0.0 58.9 %shard_map.118 = bf16[128,128]{1,0:T(8,128)(2,1)} custom-call(bf16[128,128]{1,0:T(8,128)(2,1)} %feat.1, f32[3,1024]{1,0:T(4,128)} %bitcast.6, s32[3,768]{1,0:T(4,128)} %bitcast.7, f32[768,128]{1,0:T(8,128)} %filt.1, bf16[2,128,128]{2,1,0:T(8,128)(2,1)} %mix.1, bf16[128,128]{1,0:T(8,128)(2,1)} %msgw.1, f32[1,128]{1,0:T(1,128)} %bitcast.10, ...), custom_call_target="tpu_custom_call" | custom-call | tf_op jit(solution)/shard_map/pallas_call | solution.py:402
  59.0 1.4 %copy.14 = bf16[128,128]{1,0:T(8,128)(2,1)} copy(bf16[128,128]{1,0:T(8,128)(2,1)} %shard_map.118) | data formatting | bytes 65536

commit v3 on v2

--- a/solution.py
+++ b/solution.py
@@ -93,8 +93,8 @@
 def kernel(
     zs, gs, feat, pos, wave, filt, mix, msgw, width, dist, nbr, gain, inw, outw, out,
     fall, halo, ut, ptc, pts, pc, ps, stage, acc, sc_buf, rc_buf, sy_buf, ry_buf, sz_buf, rz_buf,
-    ysrc, yall, yre, yim, es, er, msg_t,
-    know, ag_s, ag_r, ha_s, ha_r, c_s, c_r, y_s, y_r, z_s, z_r, zb_s, zb_r, yb_s, yb_r, cb_s, cb_r, e_s, e_r,
+    ysrc, yall, yre, yim, es, er, msg_t, fil_v, mix_v, inw_v, outw_v,
+    know, in_s, ag_s, ag_r, ha_s, ha_r, c_s, c_r, y_s, y_r, z_s, z_r, zb_s, zb_r, yb_s, yb_r, cb_s, cb_r, e_s, e_r,
 ):
     f32, bf16 = jnp.float32, jnp.bfloat16
     dot = functools.partial(lax.dot_general, preferred_element_type=f32)
@@ -128,24 +128,36 @@
     for device in peers:
         signal(barrier, device)
 
+    pair = ((c * 2 + yl) * zs + z) // 2
+    fetch = [
+        pltpu.make_async_copy(src, dst, in_s.at[i])
+        for i, (src, dst) in enumerate(
+            ((filt.at[pl.ds(pl.multiple_of(pair * 24, 8), 24)], fil_v), (mix, mix_v), (inw, inw_v), (outw, outw_v))
+        )
+    ]
+    for copy in fetch:
+        copy.start()
+
+    turned = [pos[:, pl.ds(pl.multiple_of(at * atoms, atoms), atoms)] for _, at in group]
     scales = lax.broadcasted_iota(jnp.int32, pos.shape, 0)
     scales = jnp.where(scales < 2, 1.0 / BOX, 1.0 / (n_dev * atoms * SLAB_STEP)).astype(f32)
-    pieces = split3(pos[...] * scales)
+    pieces = split3(jnp.concatenate(turned, axis=1) * scales)
     counts = wave[...].astype(f32).astype(bf16)
 
     pl.semaphore_wait(barrier, len(peers))
 
-    gather = []
     for o in far_first(gs):
-        copy = remote(feat, fall.at[me_g], ag_s.at[o], ag_r.at[o], group[o])
-        copy.start()
-        gather.append(copy)
+        remote(feat, fall.at[gs - o], ag_s, ag_r, group[o]).start()
     edge = atoms // 4
-    halo_up = remote(feat.at[pl.ds(atoms - edge, edge)], halo.at[0], ha_s.at[0], ha_r.at[0], up)
-    halo_down = remote(feat.at[pl.ds(0, edge)], halo.at[1], ha_s.at[1], ha_r.at[1], down)
-    halo_up.start()
-    halo_down.start()
-    fall[pl.ds(me_g, 1)] = feat[...][None]
+    remote(feat.at[pl.ds(atoms - edge, edge)], halo.at[0], ha_s, ha_r, up).start()
+    remote(feat.at[pl.ds(0, edge)], halo.at[1], ha_s, ha_r, down).start()
+    fall[0] = feat[...]
+
+    def received(ref, sem):
+        remote(ref, ref, ag_s, sem, core).wait_recv()
+
+    def sent(ref, sem):
+        remote(ref, ref, sem, ag_r, core).wait_send()
 
     steps = []
     reach = 1
@@ -184,11 +196,11 @@
     trig([(counts, p) for p in pieces], ptc, pts)
     hear(0)
     tell(1)
-
-    for copy in gather:
-        copy.wait()
+    trig([(p, counts) for p in pieces], pc, ps)
     hear(1)
     tell(2)
+    if gs > 1:
+        received(fall.at[pl.ds(1, gs - 1)], ag_r)
 
     feats = fall[...].reshape(gs * atoms, F)
 
@@ -197,32 +209,26 @@
         stage[...] = to_blocks(dot(ptc[at, :], feats, NN), dot(pts[at, :], feats, NN))
         return [stage[pl.ds(ring_z[o], 1)][0] for o in offset_of]
 
-    core_copies = []
     for i, y_at in enumerate((1 - yl, yl)):
         for s, v in enumerate(structure(1 - c, y_at)):
             sc_buf[i, s] = v.astype(bf16)
-        copy = remote(sc_buf.at[i], rc_buf.at[i], c_s.at[i], c_r.at[i], core)
-        copy.start()
-        core_copies.append(copy)
+        remote(sc_buf.at[i], rc_buf.at[i], c_s, c_r.at[i], core).start()
     cut = zs // 2
-    parts = (pl.ds(cut, zs - cut), pl.ds(0, cut))
+    parts = ((cut, zs), (0, cut))
     mine = structure(c, 1 - yl)
-    core_copies[0].wait()
-    y_copies = []
-    for i, (lo, hi) in enumerate(((cut, zs), (0, cut))):
+    received(rc_buf.at[0], c_r.at[0])
+    for i, (lo, hi) in enumerate(parts):
         for s in range(lo, hi):
             sy_buf[s] = (mine[s] + rc_buf[0, s].astype(f32)).astype(bf16)
-        copy = remote(sy_buf.at[parts[i]], ry_buf.at[parts[i]], y_s.at[i], y_r.at[i], ypeer)
-        copy.start()
-        y_copies.append(copy)
+        part = pl.ds(lo, hi - lo)
+        remote(sy_buf.at[part], ry_buf.at[part], y_s, y_r.at[i], ypeer).start()
     mine = structure(c, yl)
-    core_copies[1].wait()
+    received(rc_buf.at[1], c_r.at[1])
     for s in range(zs):
         acc[s] = mine[s] + rc_buf[1, s].astype(f32)
     hear(2)
-    ring_copies = []
-    for i, (lo, hi) in enumerate(((cut, zs), (0, cut))):
-        y_copies[i].wait()
+    for i, (lo, hi) in enumerate(parts):
+        received(ry_buf.at[pl.ds(lo, hi - lo)], y_r.at[i])
         for s in range(hi - 1, lo - 1, -1):
             total = acc[s] + ry_buf[s].astype(f32)
             if s == 0:
@@ -230,25 +236,21 @@
                 continue
             sz_buf[s] = total.astype(bf16)
             o = offset_of[s]
-            back_slot = slot_of(zs - o, zs)
-            copy = remote(sz_buf.at[s], rz_buf.at[back_slot], z_s.at[s], z_r.at[back_slot], ring[o])
-            copy.start()
-            ring_copies.append(copy)
-
-    trig([(p, counts) for p in pieces], pc, ps)
-
+            remote(sz_buf.at[s], rz_buf.at[slot_of(zs - o, zs)], z_s, z_r, ring[o]).start()
+
+    for copy in fetch:
+        copy.wait()
     total = acc[0]
-    for copy in ring_copies:
-        copy.wait()
+    others = pl.ds(1, zs - 1)
+    received(rz_buf.at[others], z_r)
     for s in range(1, zs):
         total = total + rz_buf[s].astype(f32)
 
     a = (total * (1.0 / math.sqrt(n_dev * atoms))).reshape(24, F).astype(bf16)
-    r0 = dot(a, mix[0], NN).reshape(3, 8, F)
-    r1 = dot(a, mix[1], NN).reshape(3, 8, F)
+    r0 = dot(a, mix_v[0], NN).reshape(3, 8, F)
+    r1 = dot(a, mix_v[1], NN).reshape(3, 8, F)
     odd = lax.rem(z, 2) == 1
-    pair = ((c * 2 + yl) * zs + z) // 2
-    fil = filt[pl.ds(pl.multiple_of(pair * 24, 8), 24), :].reshape(3, 8, F)
+    fil = fil_v[...].reshape(3, 8, F)
     low = low_rows((8, F))
     swapped = pltpu.roll(fil[1], 4, 0)
     f_main = jnp.where(odd, fil[2], fil[0])
@@ -265,16 +267,14 @@
     ysrc[...] = y_val
     here = c * 2 + yl
     beside = c * 2 + 1 - yl
-    back = {}
+    cuts = (0, 5, 9, 13, 16) if zs == 16 else (0, zs // 2, zs)
     for o in far_first(zs):
         s = slot_of(zs - o, zs)
-        copy = remote(ysrc, yall.at[here, s], zb_s.at[s], zb_r.at[s], ring[o])
-        copy.start()
-        back[s] = copy
+        part = sum(s >= hi for hi in cuts[1:])
+        remote(ysrc, yall.at[here, s], zb_s, zb_r.at[part], ring[o]).start()
     yall[pl.ds(here, 1), 0] = y_val[None]
 
-    halo_up.wait()
-    halo_down.wait()
+    received(halo, ha_r)
     weight = msgw[...]
     ext = jnp.concatenate(
         [
@@ -295,32 +295,18 @@
         message = message + jnp.exp(-(dist[j : j + 1, :] * inv_width)) * near
     msg_t[...] = message.T
 
-    if zs == 16:
-        cuts = (0, 5, 9, 13, 16)
-    else:
-        cuts = (0, zs // 2, zs)
-    y_back, core_back = [], []
     for i in range(len(cuts) - 1):
         lo, hi = cuts[i], cuts[i + 1]
-        for s in range(max(lo, 1), hi):
-            back[s].wait()
+        if hi > max(lo, 1):
+            received(yall.at[here, pl.ds(max(lo, 1), hi - max(lo, 1))], zb_r.at[i])
         here_part = yall.at[here, pl.ds(lo, hi - lo)]
-        copy = remote(here_part, here_part, yb_s.at[i], yb_r.at[i], ypeer)
-        copy.start()
-        y_back.append(copy)
-        copy = remote(here_part, here_part, cb_s.at[i], cb_r.at[i], core)
-        copy.start()
-        core_back.append(copy)
-        beside_part = yall.at[beside, pl.ds(lo, hi - lo)]
-        copy = remote(beside_part, beside_part, cb_s.at[4 + i], cb_r.at[4 + i], core)
-        core_back.append(copy)
-        if i > 0:
-            y_back[i - 1].wait()
-            core_back[2 * i - 1].start()
-    y_back[-1].wait()
-    core_back[-1].start()
-    for copy in core_back:
-        copy.wait()
+        remote(here_part, here_part, yb_s, yb_r.at[i], ypeer).start()
+        remote(here_part, here_part, cb_s, cb_r, core).start()
+    for i in range(len(cuts) - 1):
+        beside_part = yall.at[beside, pl.ds(cuts[i], cuts[i + 1] - cuts[i])]
+        received(beside_part, yb_r.at[i])
+        remote(beside_part, beside_part, cb_s, cb_r, core).start()
+    received(yall.at[pl.ds((1 - c) * 2, 2)], cb_r)
 
     slots = []
     for t in range(zs):
@@ -333,27 +319,36 @@
         yim[q * rows : (q + 1) * rows, :] = im.astype(bf16)
     inv_scale = 1.0 / math.sqrt(kw * gs)
 
-    def terms(g):
-        at = pl.ds(pl.multiple_of(g * atoms, atoms), atoms)
+    def terms(o):
+        at = slice(o * atoms, (o + 1) * atoms)
         return (dot(pc[at, :], yre[...], NN) + dot(ps[at, :], yim[...], NN)) * inv_scale
 
-    exchange = []
     for o in far_first(gs):
-        es[o] = terms(lax.rem(me_g + o, gs)).astype(bf16)
-        copy = remote(es.at[o], er.at[o], e_s.at[o], e_r.at[o], group[o])
-        copy.start()
-        exchange.append((o, copy))
-    ewald = terms(me_g)
-    for o, copy in exchange:
-        copy.wait()
+        es[o] = terms(o).astype(bf16)
+        remote(es.at[o], er.at[gs - o], e_s, e_r, group[o]).start()
+    ewald = terms(0)
+
+    sent(halo, ha_s)
+    sent(sc_buf, c_s)
+    sent(sy_buf, y_s)
+    sent(sz_buf.at[others], z_s)
+    sent(yall.at[here, others], zb_s)
+    sent(yall.at[here], yb_s)
+    sent(yall.at[pl.ds(c * 2, 2)], cb_s)
+    if gs > 1:
+        rest = pl.ds(1, gs - 1)
+        sent(fall.at[rest], ag_s)
+        received(er.at[rest], e_r)
+        sent(es.at[rest], e_s)
+    for o in range(1, gs):
         ewald = ewald + er[o].astype(f32)
 
     mixed = feat[...].astype(f32) + msg_t[...] + ewald
     inverse = lax.rsqrt(jnp.mean(mixed * mixed, axis=1, keepdims=True) + 1e-06)
     normed = (mixed * inverse * gain[...]).astype(bf16)
-    pre = dot(normed, inw[...], NN)
+    pre = dot(normed, inw_v[...], NN)
     hidden = (pre * (1.0 / (1.0 + jnp.exp(-pre)))).astype(bf16)
-    out[...] = (mixed + dot(hidden, outw[...], NN)).astype(bf16)
+    out[...] = (mixed + dot(hidden, outw_v[...], NN)).astype(bf16)
 
 
 def solution(mesh):
@@ -368,6 +363,7 @@
         blk = (3, 8, F)
         big = max(kw, dom)
         vm = pltpu.VMEM
+        any_, vmem = pl.BlockSpec(memory_space=pl.ANY), pl.BlockSpec(memory_space=pltpu.VMEM)
         dma = pltpu.SemaphoreType.DMA
         scratch = [
             vm((gs, atoms, F), bf16),
@@ -392,17 +388,22 @@
             vm((gs, atoms, F), bf16),
             vm((gs, atoms, F), bf16),
             vm((atoms, F), f32),
-            pltpu.SemaphoreType.REGULAR((4,)),
-            dma((gs,)), dma((gs,)), dma((2,)), dma((2,)),
-            dma((2,)), dma((2,)), dma((2,)), dma((2,)),
-            dma((zs,)), dma((zs,)), dma((zs,)), dma((zs,)),
-            dma((4,)), dma((4,)), dma((8,)), dma((8,)),
-            dma((gs,)), dma((gs,)),
+            vm((2 * WB, F), f32),
+            vm(mix_pair.shape, bf16),
+            vm(in_weight.shape, bf16),
+            vm(out_weight.shape, bf16),
+            pltpu.SemaphoreType.REGULAR((3,)),
+            dma((4,)),
+            dma, dma, dma, dma,
+            dma, dma((2,)), dma, dma((2,)),
+            dma, dma, dma, dma((4,)),
+            dma, dma((4,)), dma, dma,
+            dma, dma,
         ]
         return pl.pallas_call(
             functools.partial(kernel, zs, gs),
             out_shape=jax.ShapeDtypeStruct((atoms, F), bf16),
-            in_specs=[pl.BlockSpec(memory_space=pltpu.VMEM)] * 12,
+            in_specs=[any_ if i in (3, 4, 10, 11) else vmem for i in range(12)],
             out_specs=pl.BlockSpec(memory_space=pltpu.VMEM),
             scratch_shapes=scratch,
             compiler_params=pltpu.CompilerParams(

time: 60.5 us -> 57.8 us (0.955)
  Pallas kernels: 58.9 us -> 56.2 us
    pallas_call x1, Pallas kernels: 58.9 us -> 56.2 us  [local(): pl.pallas_call(functools.partial(kernel, zs, gs), out_shape=jax.ShapeDtyp...]
where the time goes in v3:
time: 57.8 us; the launch traced here: 57.6 us
  Pallas kernels  56.2 us (97%)
  local copies, waits for them, and re-layouts  1.38 us (2%)
    pallas_call x1, Pallas kernels, local(): pl.pallas_call(functools.partial(kernel, zs, gs), out_shape=jax.ShapeDtyp...  56.2 us
    unnamed x1, local copies, waits for them, and re-layouts  1.38 us

profile of v3, /device:TPU:1, one launch (start us, length us, event | category | flops | bytes accessed | tf_op | source)
XLA Modules:
  0.0 57.6 jit_solution(15442242020946999796)
XLA Ops:
  0.0 56.2 %shard_map.118 = bf16[128,128]{1,0:T(8,128)(2,1)} custom-call(bf16[128,128]{1,0:T(8,128)(2,1)} %feat.1, f32[3,1024]{1,0:T(4,128)} %bitcast.6, s32[3,768]{1,0:T(4,128)} %bitcast.7, f32[768,128]{1,0:T(8,128)} %filt.1, bf16[2,128,128]{2,1,0:T(8,128)(2,1)} %mix.1, bf16[128,128]{1,0:T(8,128)(2,1)} %msgw.1, f32[1,128]{1,0:T(1,128)} %bitcast.10, ...), custom_call_target="tpu_custom_call" | custom-call | tf_op jit(solution)/shard_map/pallas_call | solution.py:403
  56.2 1.4 %copy.14 = bf16[128,128]{1,0:T(8,128)(2,1)} copy(bf16[128,128]{1,0:T(8,128)(2,1)} %shard_map.118) | data formatting | bytes 65536

commit v4 on v3

--- a/solution.py
+++ b/solution.py
@@ -21,8 +21,8 @@
     r = 0.5 * np.cos(np.pi * (np.arange(4001) + 0.5) / 4001 / 2)
     t = r * r
     cheb = np.polynomial.chebyshev
-    sin_p = cheb.Chebyshev.fit(t, np.sin(np.pi * r) / r, 4, domain=[0.0, 0.25])
-    cos_p = cheb.Chebyshev.fit(t, np.cos(np.pi * r), 5, domain=[0.0, 0.25])
+    sin_p = cheb.Chebyshev.fit(t, math.sqrt(2) * np.sin(np.pi * r) / r, 4, domain=[0.0, 0.25])
+    cos_p = cheb.Chebyshev.fit(t, math.sqrt(2) * np.cos(np.pi * r), 4, domain=[0.0, 0.25])
     to = lambda p: tuple(float(v) for v in p.convert(kind=np.polynomial.Polynomial).coef)
     return to(sin_p), to(cos_p)
 
@@ -33,23 +33,20 @@
 def cos_sin_turns(u):
     r = u - jnp.round(u)
     t = r * r
-    s = jnp.full_like(t, SIN_C[-1])
-    for coef in SIN_C[-2::-1]:
+    s = t * SIN_C[-1] + SIN_C[-2]
+    for coef in SIN_C[-3::-1]:
         s = s * t + coef
     s = s * r
-    c = jnp.full_like(t, COS_C[-1])
-    for coef in COS_C[-2::-1]:
+    c = t * COS_C[-1] + COS_C[-2]
+    for coef in COS_C[-3::-1]:
         c = c * t + coef
-    s2 = s + s
-    return 1.0 - s2 * s, s2 * c
+    return 1.0 - s * s, s * c
 
 
 def split3(v):
-    hi = v.astype(jnp.bfloat16)
-    rest = v - hi.astype(jnp.float32)
-    mid = rest.astype(jnp.bfloat16)
-    low = (rest - mid.astype(jnp.float32)).astype(jnp.bfloat16)
-    return hi, mid, low
+    hi = v.astype(jnp.bfloat16).astype(jnp.float32)
+    mid = (v - hi).astype(jnp.bfloat16).astype(jnp.float32)
+    return jnp.concatenate([hi, mid, v - hi - mid], axis=0).astype(jnp.bfloat16)
 
 
 def low_rows(shape):
@@ -86,14 +83,21 @@
     return sorted(range(1, n), key=lambda o: -min(o, n - o))
 
 
+def group_order(n):
+    nx = min(4, n)
+    hops = lambda j: 2 * (j // nx) + min(j % nx, nx - j % nx)
+    back = [j // nx * nx + (nx - j % nx) % nx for j in range(n)]
+    return nx, sorted(range(1, n), key=lambda j: -hops(j)), back
+
+
 def slot_of(o, n):
     return 0 if o == 0 else 2 * o - 1 if o <= n // 2 else 2 * (n - o)
 
 
 def kernel(
     zs, gs, feat, pos, wave, filt, mix, msgw, width, dist, nbr, gain, inw, outw, out,
-    fall, halo, ut, ptc, pts, pc, ps, stage, acc, sc_buf, rc_buf, sy_buf, ry_buf, sz_buf, rz_buf,
-    ysrc, yall, yre, yim, es, er, msg_t, fil_v, mix_v, inw_v, outw_v,
+    fall, halo, ut, pt, pcs, stage, acc, sc_buf, rc_buf, sy_buf, ry_buf, sz_buf, rz_buf,
+    ysrc, yall, yv, es, er, msg_t, fil_v, mix_v, inw_v, outw_v,
     know, in_s, ag_s, ag_r, ha_s, ha_r, c_s, c_r, y_s, y_r, z_s, z_r, zb_s, zb_r, yb_s, yb_r, cb_s, cb_r, e_s, e_r,
 ):
     f32, bf16 = jnp.float32, jnp.bfloat16
@@ -105,7 +109,9 @@
     up, down = lax.rem(flat + 1, n_dev), lax.rem(flat + n_dev - 1, n_dev)
     up = (up // gs, lax.rem(up, gs))
     down = (down // gs, lax.rem(down, gs))
-    group = [(me_s, lax.rem(me_g + o, gs)) for o in range(gs)]
+    nx, group_far, group_back = group_order(gs)
+    row, col = me_g // nx, lax.rem(me_g, nx)
+    group = [(me_s, lax.rem(row + j // nx, gs // nx) * nx + lax.rem(col + j % nx, nx)) for j in range(gs)]
     core = (z * 4 + yl * 2 + 1 - c, me_g)
     ypeer = (z * 4 + (1 - yl) * 2 + c, me_g)
     ring_z = [lax.rem(z + o, zs) for o in range(zs)]
@@ -142,12 +148,13 @@
     scales = lax.broadcasted_iota(jnp.int32, pos.shape, 0)
     scales = jnp.where(scales < 2, 1.0 / BOX, 1.0 / (n_dev * atoms * SLAB_STEP)).astype(f32)
     pieces = split3(jnp.concatenate(turned, axis=1) * scales)
-    counts = wave[...].astype(f32).astype(bf16)
+    counts = wave[...].astype(f32)
+    counts = jnp.concatenate([counts, counts, counts], axis=0).astype(bf16)
 
     pl.semaphore_wait(barrier, len(peers))
 
-    for o in far_first(gs):
-        remote(feat, fall.at[gs - o], ag_s, ag_r, group[o]).start()
+    for j in group_far:
+        remote(feat, fall.at[group_back[j]], ag_s, ag_r, group[j]).start()
     edge = atoms // 4
     remote(feat.at[pl.ds(atoms - edge, edge)], halo.at[0], ha_s, ha_r, up).start()
     remote(feat.at[pl.ds(0, edge)], halo.at[1], ha_s, ha_r, down).start()
@@ -176,27 +183,21 @@
 
     tell(0)
 
-    def trig(lhs_rhs, cos_ref, sin_ref):
-        total = None
-        for lhs, rhs in lhs_rhs:
-            part = dot(lhs, rhs, TN)
-            total = part if total is None else total + part
-        n, cols = total.shape
-        ut[0:n, 0:cols] = total
-
-        def body(i, carry):
-            at = pl.ds(pl.multiple_of(i * 16, 16), 16)
-            cos_v, sin_v = cos_sin_turns(ut[at, 0:cols])
-            cos_ref[at, :] = cos_v.astype(bf16)
-            sin_ref[at, :] = sin_v.astype(bf16)
-            return carry
-
-        lax.fori_loop(0, n // 16, body, 0)
-
-    trig([(counts, p) for p in pieces], ptc, pts)
+    chunk = 16 if rows % 16 == 0 else 8
+    dom = gs * atoms
+    ut[0:kw, 0:dom] = dot(counts, pieces, TN)
+
+    @pl.loop(0, kw // chunk)
+    def _(i):
+        at = pl.ds(pl.multiple_of(i * chunk, chunk), chunk)
+        cos_v, sin_v = cos_sin_turns(ut[at, 0:dom])
+        quarter = i // (rows // chunk)
+        at = pl.ds(pl.multiple_of(lax.rem(i, rows // chunk) * chunk, chunk), chunk)
+        pt[quarter, 0, at, :] = cos_v.astype(bf16)
+        pt[quarter, 1, at, :] = sin_v.astype(bf16)
+
     hear(0)
     tell(1)
-    trig([(p, counts) for p in pieces], pc, ps)
     hear(1)
     tell(2)
     if gs > 1:
@@ -205,8 +206,8 @@
     feats = fall[...].reshape(gs * atoms, F)
 
     def structure(core_at, y_at):
-        at = pl.ds(pl.multiple_of((core_at * 2 + y_at) * rows, 8), rows)
-        stage[...] = to_blocks(dot(ptc[at, :], feats, NN), dot(pts[at, :], feats, NN))
+        sums = dot(pt[core_at * 2 + y_at].reshape(2 * rows, dom), feats, NN)
+        stage[...] = to_blocks(sums[:rows], sums[rows:])
         return [stage[pl.ds(ring_z[o], 1)][0] for o in offset_of]
 
     for i, y_at in enumerate((1 - yl, yl)):
@@ -274,6 +275,15 @@
         remote(ysrc, yall.at[here, s], zb_s, zb_r.at[part], ring[o]).start()
     yall[pl.ds(here, 1), 0] = y_val[None]
 
+    ut[0:dom, 0:kw] = dot(pieces, counts, TN)
+
+    @pl.loop(0, dom // 16)
+    def _(i):
+        at = pl.ds(pl.multiple_of(i * 16, 16), 16)
+        cos_v, sin_v = cos_sin_turns(ut[at, 0:kw])
+        pcs[at, 0:kw] = cos_v.astype(bf16)
+        pcs[at, kw : 2 * kw] = sin_v.astype(bf16)
+
     received(halo, ha_r)
     weight = msgw[...]
     ext = jnp.concatenate(
@@ -315,17 +325,16 @@
     for q in range(4):
         blocks = [yall[q, pl.ds(slots[t], 1)] for t in range(zs)]
         re, im = from_blocks(jnp.concatenate(blocks, axis=0).astype(f32))
-        yre[q * rows : (q + 1) * rows, :] = re.astype(bf16)
-        yim[q * rows : (q + 1) * rows, :] = im.astype(bf16)
+        yv[q * rows : (q + 1) * rows, :] = re.astype(bf16)
+        yv[kw + q * rows : kw + (q + 1) * rows, :] = im.astype(bf16)
     inv_scale = 1.0 / math.sqrt(kw * gs)
 
     def terms(o):
-        at = slice(o * atoms, (o + 1) * atoms)
-        return (dot(pc[at, :], yre[...], NN) + dot(ps[at, :], yim[...], NN)) * inv_scale
-
-    for o in far_first(gs):
-        es[o] = terms(o).astype(bf16)
-        remote(es.at[o], er.at[gs - o], e_s, e_r, group[o]).start()
+        return dot(pcs[o * atoms : (o + 1) * atoms, :], yv[...], NN) * inv_scale
+
+    for j in group_far:
+        es[j] = terms(j).astype(bf16)
+        remote(es.at[j], er.at[group_back[j]], e_s, e_r, group[j]).start()
     ewald = terms(0)
 
     sent(halo, ha_s)
@@ -369,10 +378,8 @@
             vm((gs, atoms, F), bf16),
             vm((2, atoms // 4, F), bf16),
             vm((big, big), f32),
-            vm((kw, dom), bf16),
-            vm((kw, dom), bf16),
-            vm((dom, kw), bf16),
-            vm((dom, kw), bf16),
+            vm((4, 2, kw // 4, dom), bf16),
+            vm((dom, 2 * kw), bf16),
             vm((zs, *blk), f32),
             vm((zs, *blk), f32),
             vm((2, zs, *blk), bf16),
@@ -383,8 +390,7 @@
             vm((zs, *blk), bf16),
             vm(blk, bf16),
             vm((4, zs, *blk), bf16),
-            vm((kw, F), bf16),
-            vm((kw, F), bf16),
+            vm((2 * kw, F), bf16),
             vm((gs, atoms, F), bf16),
             vm((gs, atoms, F), bf16),
             vm((atoms, F), f32),

time: 57.8 us -> 54.2 us (0.938)
  Pallas kernels: 56.2 us -> 52.6 us
    pallas_call x1, Pallas kernels: 56.2 us -> 52.6 us  [local(): pl.pallas_call(functools.partial(kernel, zs, gs), out_shape=jax.ShapeDtyp...]
where the time goes in v4:
time: 54.2 us; the launch traced here: 53.9 us
  Pallas kernels  52.6 us (97%)
  local copies, waits for them, and re-layouts  1.38 us (3%)
    pallas_call x1, Pallas kernels, local(): pl.pallas_call(functools.partial(kernel, zs, gs), out_shape=jax.ShapeDtyp...  52.6 us
    unnamed x1, local copies, waits for them, and re-layouts  1.38 us

profile of v4, /device:TPU:1, one launch (start us, length us, event | category | flops | bytes accessed | tf_op | source)
XLA Modules:
  0.0 53.9 jit_solution(2827205426967055554)
XLA Ops:
  0.0 52.6 %shard_map.118 = bf16[128,128]{1,0:T(8,128)(2,1)} custom-call(bf16[128,128]{1,0:T(8,128)(2,1)} %feat.1, f32[3,1024]{1,0:T(4,128)} %bitcast.6, s32[3,768]{1,0:T(4,128)} %bitcast.7, f32[768,128]{1,0:T(8,128)} %filt.1, bf16[2,128,128]{2,1,0:T(8,128)(2,1)} %mix.1, bf16[128,128]{1,0:T(8,128)(2,1)} %msgw.1, f32[1,128]{1,0:T(1,128)} %bitcast.10, ...), custom_call_target="tpu_custom_call" | custom-call | tf_op jit(solution)/shard_map/pallas_call | solution.py:409
  52.6 1.4 %copy.14 = bf16[128,128]{1,0:T(8,128)(2,1)} copy(bf16[128,128]{1,0:T(8,128)(2,1)} %shard_map.118) | data formatting | bytes 65536

commit v5 on v4

--- a/solution.py
+++ b/solution.py
@@ -95,10 +95,10 @@
 
 
 def kernel(
-    zs, gs, feat, pos, wave, filt, mix, msgw, width, dist, nbr, gain, inw, outw, out,
+    zs, gs, feat_h, pos_h, wave_h, filt_h, mix_h, msgw_h, width_h, dist_h, nbr_h, gain_h, inw_h, outw_h, out,
     fall, halo, ut, pt, pcs, stage, acc, sc_buf, rc_buf, sy_buf, ry_buf, sz_buf, rz_buf,
-    ysrc, yall, yv, es, er, msg_t, fil_v, mix_v, inw_v, outw_v,
-    know, in_s, ag_s, ag_r, ha_s, ha_r, c_s, c_r, y_s, y_r, z_s, z_r, zb_s, zb_r, yb_s, yb_r, cb_s, cb_r, e_s, e_r,
+    ysrc, yall, yv, es, er, msg_t, feat, pos, wave, filt, mix, msgw, width, dist, nbr, gain, inw, outw,
+    know, in_s, ag_s, ag_r, ha_s, ha_r, c_s, c_r, y_s, y_r, z_s, z_r, zb_s, zb_r, yb_s, yb_r, e_s, e_r,
 ):
     f32, bf16 = jnp.float32, jnp.bfloat16
     dot = functools.partial(lax.dot_general, preferred_element_type=f32)
@@ -114,6 +114,7 @@
     group = [(me_s, lax.rem(row + j // nx, gs // nx) * nx + lax.rem(col + j % nx, nx)) for j in range(gs)]
     core = (z * 4 + yl * 2 + 1 - c, me_g)
     ypeer = (z * 4 + (1 - yl) * 2 + c, me_g)
+    diagonal = (z * 4 + (1 - yl) * 2 + 1 - c, me_g)
     ring_z = [lax.rem(z + o, zs) for o in range(zs)]
     ring = [(at * 4 + yl * 2 + c, me_g) for at in ring_z]
     offset_of = sorted(range(zs), key=lambda o: slot_of(o, zs))
@@ -130,19 +131,25 @@
         pl.semaphore_signal(sem, inc=1, device_id=device, device_id_type=MESH)
 
     barrier = pltpu.get_barrier_semaphore()
-    peers = group[1:] + [up, down, core, ypeer, ring[1], ring[zs - 1]]
+    peers = group[1:] + [up, down, core, ypeer, diagonal, ring[1], ring[zs - 1]]
     for device in peers:
         signal(barrier, device)
 
     pair = ((c * 2 + yl) * zs + z) // 2
+    filt_part = filt_h.at[pl.ds(pl.multiple_of(pair * 24, 8), 24)]
     fetch = [
         pltpu.make_async_copy(src, dst, in_s.at[i])
         for i, (src, dst) in enumerate(
-            ((filt.at[pl.ds(pl.multiple_of(pair * 24, 8), 24)], fil_v), (mix, mix_v), (inw, inw_v), (outw, outw_v))
+            (
+                (pos_h, pos), (wave_h, wave), (feat_h, feat), (filt_part, filt), (mix_h, mix), (msgw_h, msgw),
+                (width_h, width), (dist_h, dist), (nbr_h, nbr), (gain_h, gain), (inw_h, inw), (outw_h, outw),
+            )
         )
     ]
     for copy in fetch:
         copy.start()
+    fetch[0].wait()
+    fetch[1].wait()
 
     turned = [pos[:, pl.ds(pl.multiple_of(at * atoms, atoms), atoms)] for _, at in group]
     scales = lax.broadcasted_iota(jnp.int32, pos.shape, 0)
@@ -151,6 +158,7 @@
     counts = wave[...].astype(f32)
     counts = jnp.concatenate([counts, counts, counts], axis=0).astype(bf16)
 
+    fetch[2].wait()
     pl.semaphore_wait(barrier, len(peers))
 
     for j in group_far:
@@ -239,7 +247,7 @@
             o = offset_of[s]
             remote(sz_buf.at[s], rz_buf.at[slot_of(zs - o, zs)], z_s, z_r, ring[o]).start()
 
-    for copy in fetch:
+    for copy in fetch[3:]:
         copy.wait()
     total = acc[0]
     others = pl.ds(1, zs - 1)
@@ -248,10 +256,10 @@
         total = total + rz_buf[s].astype(f32)
 
     a = (total * (1.0 / math.sqrt(n_dev * atoms))).reshape(24, F).astype(bf16)
-    r0 = dot(a, mix_v[0], NN).reshape(3, 8, F)
-    r1 = dot(a, mix_v[1], NN).reshape(3, 8, F)
+    r0 = dot(a, mix[0], NN).reshape(3, 8, F)
+    r1 = dot(a, mix[1], NN).reshape(3, 8, F)
     odd = lax.rem(z, 2) == 1
-    fil = fil_v[...].reshape(3, 8, F)
+    fil = filt[...].reshape(3, 8, F)
     low = low_rows((8, F))
     swapped = pltpu.roll(fil[1], 4, 0)
     f_main = jnp.where(odd, fil[2], fil[0])
@@ -267,7 +275,6 @@
     ).astype(bf16)
     ysrc[...] = y_val
     here = c * 2 + yl
-    beside = c * 2 + 1 - yl
     cuts = (0, 5, 9, 13, 16) if zs == 16 else (0, zs // 2, zs)
     for o in far_first(zs):
         s = slot_of(zs - o, zs)
@@ -310,13 +317,9 @@
         if hi > max(lo, 1):
             received(yall.at[here, pl.ds(max(lo, 1), hi - max(lo, 1))], zb_r.at[i])
         here_part = yall.at[here, pl.ds(lo, hi - lo)]
-        remote(here_part, here_part, yb_s, yb_r.at[i], ypeer).start()
-        remote(here_part, here_part, cb_s, cb_r, core).start()
-    for i in range(len(cuts) - 1):
-        beside_part = yall.at[beside, pl.ds(cuts[i], cuts[i + 1] - cuts[i])]
-        received(beside_part, yb_r.at[i])
-        remote(beside_part, beside_part, cb_s, cb_r, core).start()
-    received(yall.at[pl.ds((1 - c) * 2, 2)], cb_r)
+        for device in (diagonal, ypeer, core):
+            remote(here_part, here_part, yb_s, yb_r, device).start()
+    received(yall.at[pl.ds(1, 3)], yb_r)
 
     slots = []
     for t in range(zs):
@@ -342,8 +345,7 @@
     sent(sy_buf, y_s)
     sent(sz_buf.at[others], z_s)
     sent(yall.at[here, others], zb_s)
-    sent(yall.at[here], yb_s)
-    sent(yall.at[pl.ds(c * 2, 2)], cb_s)
+    sent(yall.at[pl.ds(1, 3)], yb_s)
     if gs > 1:
         rest = pl.ds(1, gs - 1)
         sent(fall.at[rest], ag_s)
@@ -355,9 +357,9 @@
     mixed = feat[...].astype(f32) + msg_t[...] + ewald
     inverse = lax.rsqrt(jnp.mean(mixed * mixed, axis=1, keepdims=True) + 1e-06)
     normed = (mixed * inverse * gain[...]).astype(bf16)
-    pre = dot(normed, inw_v[...], NN)
+    pre = dot(normed, inw[...], NN)
     hidden = (pre * (1.0 / (1.0 + jnp.exp(-pre)))).astype(bf16)
-    out[...] = (mixed + dot(hidden, outw_v[...], NN)).astype(bf16)
+    out[...] = (mixed + dot(hidden, outw[...], NN)).astype(bf16)
 
 
 def solution(mesh):
@@ -372,7 +374,6 @@
         blk = (3, 8, F)
         big = max(kw, dom)
         vm = pltpu.VMEM
-        any_, vmem = pl.BlockSpec(memory_space=pl.ANY), pl.BlockSpec(memory_space=pltpu.VMEM)
         dma = pltpu.SemaphoreType.DMA
         scratch = [
             vm((gs, atoms, F), bf16),
@@ -394,22 +395,29 @@
             vm((gs, atoms, F), bf16),
             vm((gs, atoms, F), bf16),
             vm((atoms, F), f32),
+            vm((atoms, F), bf16),
+            vm((3, dom), f32),
+            vm((3, kw), jnp.int32),
             vm((2 * WB, F), f32),
             vm(mix_pair.shape, bf16),
+            vm(msg_weight.shape, bf16),
+            vm((1, F), f32),
+            vm(pair_dist.shape[::-1], f32),
+            vm(neighbours.shape[::-1], jnp.int32),
+            vm((1, F), f32),
             vm(in_weight.shape, bf16),
             vm(out_weight.shape, bf16),
             pltpu.SemaphoreType.REGULAR((3,)),
-            dma((4,)),
+            dma((12,)),
             dma, dma, dma, dma,
             dma, dma((2,)), dma, dma((2,)),
             dma, dma, dma, dma((4,)),
-            dma, dma((4,)), dma, dma,
-            dma, dma,
+            dma, dma, dma, dma,
         ]
         return pl.pallas_call(
             functools.partial(kernel, zs, gs),
             out_shape=jax.ShapeDtypeStruct((atoms, F), bf16),
-            in_specs=[any_ if i in (3, 4, 10, 11) else vmem for i in range(12)],
+            in_specs=[pl.BlockSpec(memory_space=pl.ANY)] * 12,
             out_specs=pl.BlockSpec(memory_space=pltpu.VMEM),
             scratch_shapes=scratch,
             compiler_params=pltpu.CompilerParams(

time: 54.2 us -> 52.2 us (0.963)
  Pallas kernels: 52.6 us -> 50.7 us
    pallas_call x1, Pallas kernels: 52.6 us -> 50.7 us  [local(): pl.pallas_call(functools.partial(kernel, zs, gs), out_shape=jax.ShapeDtyp...]
where the time goes in v5:
time: 52.2 us; the launch traced here: 52 us
  Pallas kernels  50.7 us (97%)
  local copies, waits for them, and re-layouts  1.38 us (3%)
    pallas_call x1, Pallas kernels, local(): pl.pallas_call(functools.partial(kernel, zs, gs), out_shape=jax.ShapeDtyp...  50.7 us
    unnamed x1, local copies, waits for them, and re-layouts  1.38 us

profile of v5, /device:TPU:1, one launch (start us, length us, event | category | flops | bytes accessed | tf_op | source)
XLA Modules:
  0.0 52.0 jit_solution(2115303863946096227)
XLA Ops:
  0.0 50.7 %shard_map.118 = bf16[128,128]{1,0:T(8,128)(2,1)} custom-call(bf16[128,128]{1,0:T(8,128)(2,1)} %feat_h.1, f32[3,1024]{1,0:T(4,128)} %bitcast.6, s32[3,768]{1,0:T(4,128)} %bitcast.7, f32[768,128]{1,0:T(8,128)} %filt_h.1, bf16[2,128,128]{2,1,0:T(8,128)(2,1)} %mix_h.1, bf16[128,128]{1,0:T(8,128)(2,1)} %msgw_h.1, f32[1,128]{1,0:T(1,128)} %bitcast.10, ...), custom_call_target="tpu_custom_call" | custom-call | tf_op jit(solution)/shard_map/pallas_call | solution.py:417
  50.7 1.4 %copy.14 = bf16[128,128]{1,0:T(8,128)(2,1)} copy(bf16[128,128]{1,0:T(8,128)(2,1)} %shard_map.118) | data formatting | bytes 65536

commit v6 on v5

--- a/solution.py
+++ b/solution.py
@@ -96,9 +96,9 @@
 
 def kernel(
     zs, gs, feat_h, pos_h, wave_h, filt_h, mix_h, msgw_h, width_h, dist_h, nbr_h, gain_h, inw_h, outw_h, out,
-    fall, halo, ut, pt, pcs, stage, acc, sc_buf, rc_buf, sy_buf, ry_buf, sz_buf, rz_buf,
+    fall, halo, ut, pt, pcs, stage, acc, sc_buf, rc_buf, sz_buf, rz_buf,
     ysrc, yall, yv, es, er, msg_t, feat, pos, wave, filt, mix, msgw, width, dist, nbr, gain, inw, outw,
-    know, in_s, ag_s, ag_r, ha_s, ha_r, c_s, c_r, y_s, y_r, z_s, z_r, zb_s, zb_r, yb_s, yb_r, e_s, e_r,
+    know, in_s, ag_s, ag_r, ha_s, ha_r, c_s, c_r, z_s, z_r, zb_s, zb_r, yb_s, yb_r, e_s, e_r,
 ):
     f32, bf16 = jnp.float32, jnp.bfloat16
     dot = functools.partial(lax.dot_general, preferred_element_type=f32)
@@ -218,30 +218,32 @@
         stage[...] = to_blocks(sums[:rows], sums[rows:])
         return [stage[pl.ds(ring_z[o], 1)][0] for o in offset_of]
 
-    for i, y_at in enumerate((1 - yl, yl)):
-        for s, v in enumerate(structure(1 - c, y_at)):
-            sc_buf[i, s] = v.astype(bf16)
-        remote(sc_buf.at[i], rc_buf.at[i], c_s, c_r.at[i], core).start()
     cut = zs // 2
     parts = ((cut, zs), (0, cut))
-    mine = structure(c, 1 - yl)
-    received(rc_buf.at[0], c_r.at[0])
-    for i, (lo, hi) in enumerate(parts):
-        for s in range(lo, hi):
-            sy_buf[s] = (mine[s] + rc_buf[0, s].astype(f32)).astype(bf16)
-        part = pl.ds(lo, hi - lo)
-        remote(sy_buf.at[part], ry_buf.at[part], y_s, y_r.at[i], ypeer).start()
+    quad = (diagonal, ypeer, core)
+
+    def swap(k, i):
+        part = pl.ds(parts[i][0], parts[i][1] - parts[i][0])
+        remote(sc_buf.at[k, part], rc_buf.at[k, part], c_s, c_r.at[i], quad[k]).start()
+
+    for k, (core_at, y_at) in enumerate(((1 - c, 1 - yl), (c, 1 - yl), (1 - c, yl))):
+        for s, v in enumerate(structure(core_at, y_at)):
+            sc_buf[k, s] = v.astype(bf16)
+        swap(k, 0)
+        if k:
+            swap(k, 1)
+        if k == 1:
+            swap(0, 1)
     mine = structure(c, yl)
-    received(rc_buf.at[1], c_r.at[1])
-    for s in range(zs):
-        acc[s] = mine[s] + rc_buf[1, s].astype(f32)
     hear(2)
     for i, (lo, hi) in enumerate(parts):
-        received(ry_buf.at[pl.ds(lo, hi - lo)], y_r.at[i])
+        received(rc_buf.at[:, pl.ds(lo, hi - lo)], c_r.at[i])
         for s in range(hi - 1, lo - 1, -1):
-            total = acc[s] + ry_buf[s].astype(f32)
+            total = mine[s]
+            for k in range(3):
+                total = total + rc_buf[k, s].astype(f32)
             if s == 0:
-                acc[0] = total
+                acc[...] = total
                 continue
             sz_buf[s] = total.astype(bf16)
             o = offset_of[s]
@@ -249,7 +251,7 @@
 
     for copy in fetch[3:]:
         copy.wait()
-    total = acc[0]
+    total = acc[...]
     others = pl.ds(1, zs - 1)
     received(rz_buf.at[others], z_r)
     for s in range(1, zs):
@@ -282,7 +284,9 @@
         remote(ysrc, yall.at[here, s], zb_s, zb_r.at[part], ring[o]).start()
     yall[pl.ds(here, 1), 0] = y_val[None]
 
-    ut[0:dom, 0:kw] = dot(pieces, counts, TN)
+    send_order = group_far + [0]
+    lanes = [pieces[:, j * atoms : (j + 1) * atoms] for j in send_order]
+    ut[0:dom, 0:kw] = dot(jnp.concatenate(lanes, axis=1), counts, TN)
 
     @pl.loop(0, dom // 16)
     def _(i):
@@ -332,17 +336,20 @@
         yv[kw + q * rows : kw + (q + 1) * rows, :] = im.astype(bf16)
     inv_scale = 1.0 / math.sqrt(kw * gs)
 
-    def terms(o):
-        return dot(pcs[o * atoms : (o + 1) * atoms, :], yv[...], NN) * inv_scale
-
-    for j in group_far:
-        es[j] = terms(j).astype(bf16)
-        remote(es.at[j], er.at[group_back[j]], e_s, e_r, group[j]).start()
-    ewald = terms(0)
+    bounds = (0, 1, 4, 8) if gs == 8 else (0, gs)
+    for lo, hi in zip(bounds[:-1], bounds[1:]):
+        terms = dot(pcs[lo * atoms : hi * atoms, :], yv[...], NN) * inv_scale
+        for i in range(lo, hi):
+            j = send_order[i]
+            term = terms[(i - lo) * atoms : (i - lo + 1) * atoms]
+            if j == 0:
+                ewald = term
+                continue
+            es[j] = term.astype(bf16)
+            remote(es.at[j], er.at[group_back[j]], e_s, e_r, group[j]).start()
 
     sent(halo, ha_s)
     sent(sc_buf, c_s)
-    sent(sy_buf, y_s)
     sent(sz_buf.at[others], z_s)
     sent(yall.at[here, others], zb_s)
     sent(yall.at[pl.ds(1, 3)], yb_s)
@@ -382,11 +389,9 @@
             vm((4, 2, kw // 4, dom), bf16),
             vm((dom, 2 * kw), bf16),
             vm((zs, *blk), f32),
-            vm((zs, *blk), f32),
-            vm((2, zs, *blk), bf16),
-            vm((2, zs, *blk), bf16),
-            vm((zs, *blk), bf16),
-            vm((zs, *blk), bf16),
+            vm(blk, f32),
+            vm((3, zs, *blk), bf16),
+            vm((3, zs, *blk), bf16),
             vm((zs, *blk), bf16),
             vm((zs, *blk), bf16),
             vm(blk, bf16),
@@ -410,7 +415,7 @@
             pltpu.SemaphoreType.REGULAR((3,)),
             dma((12,)),
             dma, dma, dma, dma,
-            dma, dma((2,)), dma, dma((2,)),
+            dma, dma((2,)),
             dma, dma, dma, dma((4,)),
             dma, dma, dma, dma,
         ]

time: 52.2 us -> 52.8 us (1.011)
    pallas_call x1, Pallas kernels: 50.7 us -> 51.2 us  [local(): pl.pallas_call(functools.partial(kernel, zs, gs), out_shape=jax.ShapeDtyp...]
where the time goes in v6:
time: 52.8 us; the launch traced here: 52.6 us
  Pallas kernels  51.2 us (97%)
  local copies, waits for them, and re-layouts  1.38 us (3%)
    pallas_call x1, Pallas kernels, local(): pl.pallas_call(functools.partial(kernel, zs, gs), out_shape=jax.ShapeDtyp...  51.2 us
    unnamed x1, local copies, waits for them, and re-layouts  1.38 us

profile of v6, /device:TPU:1, one launch (start us, length us, event | category | flops | bytes accessed | tf_op | source)
XLA Modules:
  0.0 52.6 jit_solution(15523527763990872077)
XLA Ops:
  0.0 51.2 %shard_map.118 = bf16[128,128]{1,0:T(8,128)(2,1)} custom-call(bf16[128,128]{1,0:T(8,128)(2,1)} %feat_h.1, f32[3,1024]{1,0:T(4,128)} %bitcast.6, s32[3,768]{1,0:T(4,128)} %bitcast.7, f32[768,128]{1,0:T(8,128)} %filt_h.1, bf16[2,128,128]{2,1,0:T(8,128)(2,1)} %mix_h.1, bf16[128,128]{1,0:T(8,128)(2,1)} %msgw_h.1, f32[1,128]{1,0:T(1,128)} %bitcast.10, ...), custom_call_target="tpu_custom_call" | custom-call | tf_op jit(solution)/shard_map/pallas_call | solution.py:422
  51.2 1.4 %copy.14 = bf16[128,128]{1,0:T(8,128)(2,1)} copy(bf16[128,128]{1,0:T(8,128)(2,1)} %shard_map.118) | data formatting | bytes 65536

commit v7 on v5

--- a/solution.py
+++ b/solution.py
@@ -218,17 +218,21 @@
         stage[...] = to_blocks(sums[:rows], sums[rows:])
         return [stage[pl.ds(ring_z[o], 1)][0] for o in offset_of]
 
-    for i, y_at in enumerate((1 - yl, yl)):
+    def to_core(i, y_at):
         for s, v in enumerate(structure(1 - c, y_at)):
             sc_buf[i, s] = v.astype(bf16)
         remote(sc_buf.at[i], rc_buf.at[i], c_s, c_r.at[i], core).start()
-    cut = zs // 2
-    parts = ((cut, zs), (0, cut))
+
+    to_core(0, 1 - yl)
     mine = structure(c, 1 - yl)
+    for s in range(zs):
+        acc[s] = mine[s]
+    to_core(1, yl)
+    parts = ((12, 16), (6, 12), (0, 6)) if zs == 16 else ((zs // 2, zs), (0, zs // 2))
     received(rc_buf.at[0], c_r.at[0])
     for i, (lo, hi) in enumerate(parts):
         for s in range(lo, hi):
-            sy_buf[s] = (mine[s] + rc_buf[0, s].astype(f32)).astype(bf16)
+            sy_buf[s] = (acc[s] + rc_buf[0, s].astype(f32)).astype(bf16)
         part = pl.ds(lo, hi - lo)
         remote(sy_buf.at[part], ry_buf.at[part], y_s, y_r.at[i], ypeer).start()
     mine = structure(c, yl)
@@ -275,14 +279,16 @@
     ).astype(bf16)
     ysrc[...] = y_val
     here = c * 2 + yl
-    cuts = (0, 5, 9, 13, 16) if zs == 16 else (0, zs // 2, zs)
+    cuts = (0, 5, 9, 13, 15, 16) if zs == 16 else (0, zs // 2, zs)
     for o in far_first(zs):
         s = slot_of(zs - o, zs)
         part = sum(s >= hi for hi in cuts[1:])
         remote(ysrc, yall.at[here, s], zb_s, zb_r.at[part], ring[o]).start()
     yall[pl.ds(here, 1), 0] = y_val[None]
 
-    ut[0:dom, 0:kw] = dot(pieces, counts, TN)
+    send_order = group_far + [0]
+    lanes = [pieces[:, j * atoms : (j + 1) * atoms] for j in send_order]
+    ut[0:dom, 0:kw] = dot(jnp.concatenate(lanes, axis=1), counts, TN)
 
     @pl.loop(0, dom // 16)
     def _(i):
@@ -332,13 +338,17 @@
         yv[kw + q * rows : kw + (q + 1) * rows, :] = im.astype(bf16)
     inv_scale = 1.0 / math.sqrt(kw * gs)
 
-    def terms(o):
-        return dot(pcs[o * atoms : (o + 1) * atoms, :], yv[...], NN) * inv_scale
-
-    for j in group_far:
-        es[j] = terms(j).astype(bf16)
-        remote(es.at[j], er.at[group_back[j]], e_s, e_r, group[j]).start()
-    ewald = terms(0)
+    bounds = (0, 1, 4, 8) if gs == 8 else (0, gs)
+    for lo, hi in zip(bounds[:-1], bounds[1:]):
+        terms = dot(pcs[lo * atoms : hi * atoms, :], yv[...], NN) * inv_scale
+        for i in range(lo, hi):
+            j = send_order[i]
+            term = terms[(i - lo) * atoms : (i - lo + 1) * atoms]
+            if j == 0:
+                ewald = term
+                continue
+            es[j] = term.astype(bf16)
+            remote(es.at[j], er.at[group_back[j]], e_s, e_r, group[j]).start()
 
     sent(halo, ha_s)
     sent(sc_buf, c_s)
@@ -410,8 +420,8 @@
             pltpu.SemaphoreType.REGULAR((3,)),
             dma((12,)),
             dma, dma, dma, dma,
-            dma, dma((2,)), dma, dma((2,)),
-            dma, dma, dma, dma((4,)),
+            dma, dma((2,)), dma, dma((3,)),
+            dma, dma, dma, dma((5,)),
             dma, dma, dma, dma,
         ]
         return pl.pallas_call(

time: 52.2 us -> 53.8 us (1.031)
  Pallas kernels: 50.7 us -> 52.2 us
    pallas_call x1, Pallas kernels: 50.7 us -> 52.2 us  [local(): pl.pallas_call(functools.partial(kernel, zs, gs), out_shape=jax.ShapeDtyp...]
where the time goes in v7:
time: 53.8 us; the launch traced here: 53.6 us
  Pallas kernels  52.2 us (97%)
  local copies, waits for them, and re-layouts  1.38 us (3%)
    pallas_call x1, Pallas kernels, local(): pl.pallas_call(functools.partial(kernel, zs, gs), out_shape=jax.ShapeDtyp...  52.2 us
    unnamed x1, local copies, waits for them, and re-layouts  1.38 us

profile of v7, /device:TPU:1, one launch (start us, length us, event | category | flops | bytes accessed | tf_op | source)
XLA Modules:
  0.0 53.6 jit_solution(13331729449997392877)
XLA Ops:
  0.0 52.2 %shard_map.118 = bf16[128,128]{1,0:T(8,128)(2,1)} custom-call(bf16[128,128]{1,0:T(8,128)(2,1)} %feat_h.1, f32[3,1024]{1,0:T(4,128)} %bitcast.6, s32[3,768]{1,0:T(4,128)} %bitcast.7, f32[768,128]{1,0:T(8,128)} %filt_h.1, bf16[2,128,128]{2,1,0:T(8,128)(2,1)} %mix_h.1, bf16[128,128]{1,0:T(8,128)(2,1)} %msgw_h.1, f32[1,128]{1,0:T(1,128)} %bitcast.10, ...), custom_call_target="tpu_custom_call" | custom-call | tf_op jit(solution)/shard_map/pallas_call | solution.py:427
  52.2 1.4 %copy.14 = bf16[128,128]{1,0:T(8,128)(2,1)} copy(bf16[128,128]{1,0:T(8,128)(2,1)} %shard_map.118) | data formatting | bytes 65536

commit v8 on v6

--- a/solution.py
+++ b/solution.py
@@ -230,10 +230,7 @@
         for s, v in enumerate(structure(core_at, y_at)):
             sc_buf[k, s] = v.astype(bf16)
         swap(k, 0)
-        if k:
-            swap(k, 1)
-        if k == 1:
-            swap(0, 1)
+        swap(k, 1)
     mine = structure(c, yl)
     hear(2)
     for i, (lo, hi) in enumerate(parts):

time: 52.8 us -> 51.9 us (0.983)
  Pallas kernels: 51.2 us -> 50.3 us
    pallas_call x1, Pallas kernels: 51.2 us -> 50.3 us  [local(): pl.pallas_call(functools.partial(kernel, zs, gs), out_shape=jax.ShapeDtyp...]
where the time goes in v8:
time: 51.9 us; the launch traced here: 51.7 us
  Pallas kernels  50.3 us (97%)
  local copies, waits for them, and re-layouts  1.38 us (3%)
    pallas_call x1, Pallas kernels, local(): pl.pallas_call(functools.partial(kernel, zs, gs), out_shape=jax.ShapeDtyp...  50.3 us
    unnamed x1, local copies, waits for them, and re-layouts  1.38 us

profile of v8, /device:TPU:1, one launch (start us, length us, event | category | flops | bytes accessed | tf_op | source)
XLA Modules:
  0.0 51.7 jit_solution(13656478884862331639)
XLA Ops:
  0.0 50.3 %shard_map.118 = bf16[128,128]{1,0:T(8,128)(2,1)} custom-call(bf16[128,128]{1,0:T(8,128)(2,1)} %feat_h.1, f32[3,1024]{1,0:T(4,128)} %bitcast.6, s32[3,768]{1,0:T(4,128)} %bitcast.7, f32[768,128]{1,0:T(8,128)} %filt_h.1, bf16[2,128,128]{2,1,0:T(8,128)(2,1)} %mix_h.1, bf16[128,128]{1,0:T(8,128)(2,1)} %msgw_h.1, f32[1,128]{1,0:T(1,128)} %bitcast.10, ...), custom_call_target="tpu_custom_call" | custom-call | tf_op jit(solution)/shard_map/pallas_call | solution.py:419
  50.4 1.4 %copy.14 = bf16[128,128]{1,0:T(8,128)(2,1)} copy(bf16[128,128]{1,0:T(8,128)(2,1)} %shard_map.118) | data formatting | bytes 65536

commit v9 on v8

--- a/solution.py
+++ b/solution.py
@@ -219,6 +219,7 @@
         return [stage[pl.ds(ring_z[o], 1)][0] for o in offset_of]
 
     cut = zs // 2
+    cut = 11 if zs == 16 else cut
     parts = ((cut, zs), (0, cut))
     quad = (diagonal, ypeer, core)
 

time: 51.9 us -> 51.9 us (level)
  no operation moved by 1% of the time
where the time goes in v9:
time: 51.9 us; the launch traced here: 51.8 us
  Pallas kernels  50.4 us (97%)
  local copies, waits for them, and re-layouts  1.38 us (3%)
    pallas_call x1, Pallas kernels, local(): pl.pallas_call(functools.partial(kernel, zs, gs), out_shape=jax.ShapeDtyp...  50.4 us
    unnamed x1, local copies, waits for them, and re-layouts  1.38 us

profile of v9, /device:TPU:1, one launch (start us, length us, event | category | flops | bytes accessed | tf_op | source)
XLA Modules:
  0.0 51.8 jit_solution(3305875813955016629)
XLA Ops:
  0.0 50.4 %shard_map.118 = bf16[128,128]{1,0:T(8,128)(2,1)} custom-call(bf16[128,128]{1,0:T(8,128)(2,1)} %feat_h.1, f32[3,1024]{1,0:T(4,128)} %bitcast.6, s32[3,768]{1,0:T(4,128)} %bitcast.7, f32[768,128]{1,0:T(8,128)} %filt_h.1, bf16[2,128,128]{2,1,0:T(8,128)(2,1)} %mix_h.1, bf16[128,128]{1,0:T(8,128)(2,1)} %msgw_h.1, f32[1,128]{1,0:T(1,128)} %bitcast.10, ...), custom_call_target="tpu_custom_call" | custom-call | tf_op jit(solution)/shard_map/pallas_call | solution.py:420
  50.4 1.4 %copy.14 = bf16[128,128]{1,0:T(8,128)(2,1)} copy(bf16[128,128]{1,0:T(8,128)(2,1)} %shard_map.118) | data formatting | bytes 65536
